TPU v7x, 32 devices: a whole 2x2x4 slice. The times are simulated.
32 devices in a mesh: tm: 4 (over y, core), height: 4 (over z), width: 2 (over x).
Axes of the slice: x: 2, y: 2, z: 4, core: 2. Of those that a mesh axis runs over, the one named last changes fastest.
Arguments:
- tokens: bfloat16 [2048, 3072], P(('tm', 'height', 'width'))
- shift_mod: float32 [3072], replicated, may hold values from -3 to 3
- scale_mod: float32 [3072], replicated, may hold values from -2.5 to 2.5
- proj_weight: bfloat16 [64, 3072], replicated, may hold values from -0.109375 to 0.109375
- proj_bias: float32 [64], replicated, may hold values from -3 to 3
- conv1_weight: bfloat16 [3, 3, 3, 16, 512], replicated, may hold values from -0.3125 to 0.3125
- conv1_bias: float32 [512], replicated, may hold values from -3 to 3
- norm_gain: float32 [512], replicated, may hold values from 0.25 to 1.75
- norm_bias: float32 [512], replicated, may hold values from -3 to 3
- conv2_weight: bfloat16 [3, 3, 3, 512, 512], P(None, None, None, 'width'), may hold values from -0.0546875 to 0.0546875
- conv2_bias: float32 [512], replicated, may hold values from -3 to 3
Outputs:
- pixels: bfloat16 [16, 32, 16, 512], P('tm', 'height', 'width')
All inputs are finite; a program needn't handle non-finite values.
Results may differ from a plain program's by a relative error of at most 0.0095.
Values may be sent and summed in bfloat16 or wider, within the bound.
No kernel may reach another device: no remote copies, remote signals or barrier semaphores. Data moves between devices by JAX's collectives and lax.ppermute only.
A program may use at most 128 MiB of HBM per device.

v0:
```python
import jax
import jax.numpy as jnp
from jax import lax
from jax.sharding import PartitionSpec as P

LAT = 16
C1 = 512
GROUPS = 32
FT = 4
TH = 8
TW = 8
PF = 64


def with_halo(x, sides, width):
    for axis, dim in sides:
        peers, length = (lax.axis_size(axis), x.shape[dim])
        up = [(i, (i + 1) % peers) for i in range(peers - 1)]
        down = [(j, i) for i, j in up]
        last = lax.slice_in_dim(x, length - width, length, axis=dim)
        leading = lax.slice_in_dim(x, 0, width, axis=dim)
        before = lax.ppermute(last, axis, up)
        after = lax.ppermute(leading, axis, down)
        x = jnp.concatenate([before, x, after], axis=dim)
    return x


def shifted(value, axis, steps):
    count = lax.axis_size(axis)
    leading, last = (max(0, -steps), min(count, count - steps))
    return lax.ppermute(value, axis, [(source, source + steps) for source in range(leading, last)])


def project(values_in, shift_mod, scale_mod, proj_weight, proj_bias):
    values = values_in.astype(jnp.float32)
    center = jnp.mean(values, axis=-1, keepdims=True)
    spread = jnp.mean((values - center) * (values - center), axis=-1, keepdims=True)
    normed = ((values - center) * lax.rsqrt(spread + 1e-06) * (1.0 + scale_mod) + shift_mod).astype(
        jnp.bfloat16
    )
    projected = lax.dot_general(
        normed, proj_weight, (((1,), (1,)), ((), ())), preferred_element_type=jnp.float32
    )
    result = (projected + proj_bias).astype(jnp.bfloat16)
    return result


def convolve(padded, weight, frames, rows, cols):
    channels = weight.shape[3]
    outputs = weight.shape[4]
    total = jnp.zeros((frames * rows * cols, outputs), jnp.float32)
    for row_tap in range(3):
        for col_tap in range(3):
            window = jnp.concatenate(
                [
                    padded[
                        frame_tap : frame_tap + frames,
                        row_tap : row_tap + rows,
                        col_tap : col_tap + cols,
                        :,
                    ]
                    for frame_tap in range(3)
                ],
                axis=-1,
            )
            taps = weight[:, row_tap, col_tap].reshape(3 * channels, outputs)
            total = total + jnp.dot(
                window.reshape(-1, 3 * channels), taps, preferred_element_type=jnp.float32
            )
    return total.reshape(frames, rows, cols, outputs)


def per_device(
    tokens,
    shift_mod,
    scale_mod,
    proj_weight,
    proj_bias,
    conv1_weight,
    conv1_bias,
    norm_gain,
    norm_bias,
    conv2_weight,
    conv2_bias,
):
    width_count = lax.axis_size("width")
    height_count = lax.axis_size("height")
    time_count = lax.axis_size("tm")
    line_rows = FT * TH // (2 * width_count)
    half_rows = TH // 2
    half_cols = TW // 2
    local_patches = project(tokens, shift_mod, scale_mod, proj_weight, proj_bias)
    sectioned = local_patches.reshape(line_rows, width_count, half_cols, PF)
    sectioned = lax.all_to_all(sectioned, "width", split_axis=1, concat_axis=0, tiled=True)
    sectioned = sectioned.reshape(FT // height_count, height_count, half_rows, half_cols, PF)
    sectioned = lax.all_to_all(sectioned, "height", split_axis=1, concat_axis=0, tiled=True)
    patches = sectioned.reshape(FT, half_rows, half_cols, PF)
    latent = (
        patches.reshape(FT, half_rows, half_cols, LAT, 2, 2)
        .transpose(0, 1, 4, 2, 5, 3)
        .reshape(FT, TH, TW, LAT)
    )
    group_size = C1 // GROUPS
    count = FT * TH * TW * time_count * height_count * width_count * group_size
    padded = with_halo(latent, (("height", 1), ("width", 2)), 2)
    earlier = shifted(padded, "tm", 1)
    stacked = jnp.concatenate([earlier, padded], axis=0)
    hidden = (convolve(stacked, conv1_weight, FT + 2, TH + 2, TW + 2) + conv1_bias).astype(
        jnp.bfloat16
    )
    grouped = hidden[2:, 1:-1, 1:-1].astype(jnp.float32).reshape(-1, GROUPS, group_size)
    sums = jnp.sum(grouped, axis=(0, 2))
    squares = jnp.sum(grouped * grouped, axis=(0, 2))
    sums, squares = lax.psum((sums, squares), ("tm", "height", "width"))
    gmean = sums / count
    gvar = squares / count - gmean * gmean
    mean_full = jnp.repeat(gmean, group_size)
    inverse_full = jnp.repeat(lax.rsqrt(gvar + 1e-06), group_size)
    scaled = (hidden.astype(jnp.float32) - mean_full) * inverse_full * norm_gain + norm_bias
    activated = jax.nn.silu(scaled).astype(jnp.bfloat16)
    frame_global = lax.axis_index("tm") * FT - 2 + jnp.arange(FT + 2)
    row_global = lax.axis_index("height") * TH - 1 + jnp.arange(TH + 2)
    col_global = lax.axis_index("width") * TW - 1 + jnp.arange(TW + 2)
    frame_valid = frame_global >= 0
    row_valid = (row_global >= 0) & (row_global < TH * height_count)
    col_valid = (col_global >= 0) & (col_global < TW * width_count)
    inside = (
        frame_valid[:, None, None, None]
        & row_valid[None, :, None, None]
        & col_valid[None, None, :, None]
    )
    act_stacked = jnp.where(inside, activated, jnp.zeros_like(activated))
    total = convolve(
        act_stacked, lax.all_gather(conv2_weight, "width", axis=3, tiled=True), FT, TH, TW
    )
    return (total + conv2_bias).astype(jnp.bfloat16)


def solution(mesh):
    placed = (
        P(("tm", "height", "width"), None),
        P(),
        P(),
        P(),
        P(),
        P(),
        P(),
        P(),
        P(),
        P(None, None, None, "width", None),
        P(),
    )
    return jax.shard_map(
        per_device,
        mesh=mesh,
        in_specs=placed,
        out_specs=P("tm", "height", "width", None),
        check_vma=False,
    )
```

profile of v0, /device:TPU:0, one launch (start us, length us, event | category | flops | bytes accessed | tf_op | source)
XLA Modules:
  0.0 205.0 jit_solution(6254833569561330727)
XLA Ops:
  6.6 0.7 all-gather.2.cloned.1.call-update
  8.5 0.7 reshape.178
  9.1 4.2 %all-to-all-start = ((bf16[2,2,1024]{2,1,0:T(2,128)(2,1)}), bf16[2,2,1024]{2,1,0:T(2,128)(2,1)S(1)}, u32[]{:S(2)}, u32[]{:S(2)}) async-start(bf16[2,2,1024]{2,1,0:T(2,128)(2,1)} %reshape.178), calls=%async_computation | async-start | bytes 16384 | tf_op jit(solution)/shard_map/all_to_all | solution.py:94
  13.4 0.8 fusion.17
  14.1 3.1 %all-to-all-done = bf16[2,2,1024]{2,1,0:T(2,128)(2,1)S(1)} async-done(((bf16[2,2,1024]{2,1,0:T(2,128)(2,1)}), bf16[2,2,1024]{2,1,0:T(2,128)(2,1)S(1)}, u32[]{:S(2)}, u32[]{:S(2)}) %all-to-all-start) | async-done | bytes 8224 | tf_op jit(solution)/shard_map/all_to_all | solution.py:94
  17.3 0.7 reshape.180
  18.0 5.3 %all-to-all-start.1 = ((bf16[4,2,512]{2,1,0:T(2,128)(2,1)}), bf16[4,2,512]{2,1,0:T(2,128)(2,1)S(1)}, u32[]{:S(2)}, u32[]{:S(2)}) async-start(bf16[4,2,512]{2,1,0:T(2,128)(2,1)} %reshape.180), calls=%async_computation.1 | async-start | bytes 16384 | tf_op jit(solution)/shard_map/all_to_all | solution.py:96
  23.3 5.6 %all-to-all-done.1 = bf16[4,2,512]{2,1,0:T(2,128)(2,1)S(1)} async-done(((bf16[4,2,512]{2,1,0:T(2,128)(2,1)}), bf16[4,2,512]{2,1,0:T(2,128)(2,1)S(1)}, u32[]{:S(2)}, u32[]{:S(2)}) %all-to-all-start.1) | async-done | bytes 8224 | tf_op jit(solution)/shard_map/all_to_all | solution.py:96
  29.7 2.5 %collective-permute-start = (bf16[4,2,8,16]{3,2,1,0:T(8,128)(2,1)S(1)}, bf16[4,2,8,16]{3,2,1,0:T(8,128)(2,1)S(1)}, u32[]{:S(2)}, u32[]{:S(2)}) collective-permute-start(bf16[4,2,8,16]{3,2,1,0:T(8,128)(2,1)S(1)} %get-tuple-element.83), channel_id=1, source_target_pairs={{0,2},{2,4},{4,6},{1,3},{3,5},{5,7},{8,10},{10,12},{12,14},{9,11},... | collective-permute-start | bytes 6152 | tf_op jit(solution)/shard_map/ppermute | solution.py:22
  32.2 1.3 collective-permute-start.1
  33.7 4.2 %collective-permute-done.1 = bf16[4,2,8,16]{3,2,1,0:T(8,128)(2,1)S(1)} collective-permute-done((bf16[4,2,8,16]{3,2,1,0:T(8,128)(2,1)S(1)}, bf16[4,2,8,16]{3,2,1,0:T(8,128)(2,1)S(1)}, u32[]{:S(2)}, u32[]{:S(2)}) %collective-permute-start.1) | collective-permute-done | bytes 2080 | tf_op jit(solution)/shard_map/ppermute | solution.py:23
  37.9 1.9 collective-permute-start.2
  39.8 1.3 collective-permute-start.3
  41.2 0.6 collective-permute-done.2
  41.8 4.4 %collective-permute-done.3 = bf16[4,12,2,16]{3,2,1,0:T(2,128)(2,1)S(1)} collective-permute-done((bf16[4,12,2,16]{3,2,1,0:T(2,128)(2,1)S(1)}, bf16[4,12,2,16]{3,2,1,0:T(2,128)(2,1)S(1)}, u32[]{:S(2)}, u32[]{:S(2)}) %collective-permute-start.3) | collective-permute-done | bytes 3104 | tf_op jit(solution)/shard_map/ppermute | solution.py:23
  46.3 1.3 collective-permute-start.4
  47.7 1.0 collective-permute-done.4
  48.8 1.1 fusion.19
  50.4 0.7 reshape.158
  51.1 0.7 reshape.159
  51.9 1.6 fusion.18
  53.8 2.7 %pad_maximum_fusion.11 = (bf16[6,10,10,48]{3,2,1,0:T(8,128)(2,1)}, bf16[6,10,10,48]{3,2,1,0:T(8,128)(2,1)S(1)}) fusion(bf16[6,10,10,16]{3,2,1,0:T(8,128)(2,1)} %get-tuple-element.72, bf16[6,10,10,16]{3,2,1,0:T(8,128)(2,1)} %get-tuple-element.74, bf16[6,10,10,16]{3,2,1,0:T(8,128)(2,1)} %get-tuple-element.73, bf16[6,10,10,16]{3,2,1,0:T(8,128)(2,1)} %get-tuple-element.69, ...), kind=kLoop, calls=%fused_computation.49 | loop fusion | flops 345600 | bytes 230400 | tf_op jit(solution)/shard_map/concatenate | solution.py:54
  56.5 1.7 reshape.160
  58.2 0.8 reshape.161
  58.9 1.2 pad_maximum_fusion.15
  60.1 1.0 reshape.164
  66.4 1.3 convolution_add_fusion
  67.7 1.4 reshape.167
  70.1 43.8 %all-reduce = (f32[32]{0:T(128)S(1)}, f32[32]{0:T(128)S(1)}) all-reduce(f32[32]{0:T(128)S(1)} %reduce_sum.57, f32[32]{0:T(128)S(1)} %reduce_sum.54), channel_id=1, replica_groups=mesh['tm'=4,'height'=4,'width'=2] {'tm','height','width'}, use_global_device_ids=true, to_apply=%region_7.8 | all-reduce | flops 64 | bytes 512 | tf_op jit(solution)/shard_map/psum | solution.py:114
  114.2 0.8 fusion.1
  115.4 0.8 fusion.15
  116.2 1.0 pad_maximum_fusion.2
  117.2 1.0 pad_maximum_fusion.6
  118.2 0.9 pad_maximum_fusion.5
  119.1 1.0 pad_maximum_fusion.4
  120.1 1.0 pad_maximum_fusion.3
  121.1 62.3 %all-gather.2.cloned.1.call-done = bf16[3,3,3,512,512]{4,3,2,1,0:T(8,128)(2,1)} async-done(((bf16[3,3,3,256,512]{4,3,2,1,0:T(8,128)(2,1)}), bf16[3,3,3,512,512]{4,3,2,1,0:T(8,128)(2,1)}) %all-gather.2.cloned.1.call-update) | async-done | bytes 14155792 | tf_op jit(solution)/shard_map/all_gather | solution.py:134
  183.4 5.9 %fusion.14 = (bf16[3,1,1,512,512]{4,3,2,1,0:T(8,128)(2,1)S(1)}, bf16[3,1,1,512,512]{4,3,2,1,0:T(8,128)(2,1)S(1)}, bf16[3,1,1,512,512]{4,3,2,1,0:T(8,128)(2,1)S(1...) fusion(bf16[3,3,3,512,512]{4,3,2,1,0:T(8,128)(2,1)} %all-gather, ...), kind=kLoop, calls=%fused_computation.70 | loop fusion | bytes 28311552 | tf_op jit(solution)/shard_map/slice | solution.py:66
  189.3 0.6 fusion.22
  189.9 0.6 convolution_add_fusion.15
  191.0 0.6 convolution_add_fusion.14
  192.1 0.6 convolution_add_fusion.13
  193.3 0.6 convolution_add_fusion.12
  194.4 0.6 convolution_add_fusion.11
  195.5 0.6 convolution_add_fusion.10
  196.1 0.6 convolution_add_fusion.9
  196.7 0.6 convolution_add_fusion.8
  197.4 0.7 add_convert_fusion.1
  (109 shorter events, 13.1 us)
Async XLA Ops:
  6.5 1.5 copy-start
  6.5 1.0 copy-start.7
  6.5 1.5 copy-start.20
  6.5 1.5 copy-start.26
  6.5 1.5 copy-start.25
  6.5 176.8 %all-gather.2.cloned.1.call-start = ((), (), s32[]{:S(2)}) async-start(), calls=%async_computation.2 | async-start | bytes 21233664 | tf_op jit(solution)/shard_map/all_gather | solution.py:134
  7.6 5.8 %copy-start.12 = (bf16[3,3,3,16,512]{4,3,2,1,0:T(8,128)(2,1)S(1)}, bf16[3,3,3,16,512]{4,3,2,1,0:T(8,128)(2,1)}, u32[]{:S(2)}) copy-start(bf16[3,3,3,16,512]{4,3,2,1,0:T(8,128)(2,1)} %param.16) | copy-start | bytes 1327108
  9.1 8.1 %all-to-all-start = ((bf16[2,2,1024]{2,1,0:T(2,128)(2,1)}), bf16[2,2,1024]{2,1,0:T(2,128)(2,1)S(1)}, u32[]{:S(2)}, u32[]{:S(2)}) async-start(bf16[2,2,1024]{2,1,0:T(2,128)(2,1)} %reshape.178), calls=%async_computation | async-start | bytes 16384 | tf_op jit(solution)/shard_map/all_to_all | solution.py:94
  18.0 10.9 %all-to-all-start.1 = ((bf16[4,2,512]{2,1,0:T(2,128)(2,1)}), bf16[4,2,512]{2,1,0:T(2,128)(2,1)S(1)}, u32[]{:S(2)}, u32[]{:S(2)}) async-start(bf16[4,2,512]{2,1,0:T(2,128)(2,1)} %reshape.180), calls=%async_computation.1 | async-start | bytes 16384 | tf_op jit(solution)/shard_map/all_to_all | solution.py:96
  29.7 4.0 %collective-permute-start = (bf16[4,2,8,16]{3,2,1,0:T(8,128)(2,1)S(1)}, bf16[4,2,8,16]{3,2,1,0:T(8,128)(2,1)S(1)}, u32[]{:S(2)}, u32[]{:S(2)}) collective-permute-start(bf16[4,2,8,16]{3,2,1,0:T(8,128)(2,1)S(1)} %get-tuple-element.83), channel_id=1, source_target_pairs={{0,2},{2,4},{4,6},{1,3},{3,5},{5,7},{8,10},{10,12},{12,14},{9,11},... | collective-permute-start | bytes 6152 | tf_op jit(solution)/shard_map/ppermute | solution.py:22
  32.2 5.6 %collective-permute-start.1 = (bf16[4,2,8,16]{3,2,1,0:T(8,128)(2,1)S(1)}, bf16[4,2,8,16]{3,2,1,0:T(8,128)(2,1)S(1)}, u32[]{:S(2)}, u32[]{:S(2)}) collective-permute-start(bf16[4,2,8,16]{3,2,1,0:T(8,128)(2,1)S(1)} %get-tuple-element.84), channel_id=1, source_target_pairs={{2,0},{4,2},{6,4},{3,1},{5,3},{7,5},{10,8},{12,10},{14,12},{11,9},... | collective-permute-start | bytes 6152 | tf_op jit(solution)/shard_map/ppermute | solution.py:23
  37.9 3.9 %collective-permute-start.2 = (bf16[4,12,2,16]{3,2,1,0:T(2,128)(2,1)S(1)}, bf16[4,12,2,16]{3,2,1,0:T(2,128)(2,1)S(1)}, u32[]{:S(2)}, u32[]{:S(2)}) collective-permute-start(bf16[4,12,2,16]{3,2,1,0:T(2,128)(2,1)S(1)} %get-tuple-element.81), channel_id=1, source_target_pairs={{0,1},{2,3},{4,5},{6,7},{8,9},{10,11},{12,13},{14,15},{16,17},{18,... | collective-permute-start | bytes 9224 | tf_op jit(solution)/shard_map/ppermute | solution.py:22
  39.8 6.4 %collective-permute-start.3 = (bf16[4,12,2,16]{3,2,1,0:T(2,128)(2,1)S(1)}, bf16[4,12,2,16]{3,2,1,0:T(2,128)(2,1)S(1)}, u32[]{:S(2)}, u32[]{:S(2)}) collective-permute-start(bf16[4,12,2,16]{3,2,1,0:T(2,128)(2,1)S(1)} %get-tuple-element.82), channel_id=1, source_target_pairs={{1,0},{3,2},{5,4},{7,6},{9,8},{11,10},{13,12},{15,14},{17,16},{19,... | collective-permute-start | bytes 9224 | tf_op jit(solution)/shard_map/ppermute | solution.py:23
  46.3 2.4 %collective-permute-start.4 = (bf16[4,12,12,16]{3,2,1,0:T(8,128)(2,1)S(1)}, bf16[4,12,12,16]{3,2,1,0:T(8,128)(2,1)S(1)}, u32[]{:S(2)}, u32[]{:S(2)}) collective-permute-start(bf16[4,12,12,16]{3,2,1,0:T(8,128)(2,1)S(1)} %pad_maximum_fusion.18), channel_id=1, source_target_pairs={{0,8},{8,16},{16,24},{1,9},{9,17},{17,25},{2,10},{10,18},{18,26},{... | collective-permute-start | bytes 55304 | tf_op jit(solution)/shard_map/ppermute | solution.py:31
  61.1 0.9 copy-start.8
  61.7 0.9 copy-start.9
  61.7 0.9 copy-start.19
  62.3 0.9 copy-start.11
  62.3 0.9 copy-start.18
  63.0 0.9 copy-start.10
  63.0 0.9 copy-start.17
  63.6 0.8 copy-start.16
  64.2 0.8 copy-start.15
  64.7 0.8 copy-start.14
  65.3 0.8 copy-start.13
  67.7 1.4 copy-start.21
  69.1 45.1 %copy-start.22 = (f32[512]{0:T(512)S(1)}, f32[512]{0:T(512)}, u32[]{:S(2)}) copy-start(f32[512]{0:T(512)} %param.19) | copy-start | bytes 6148
  69.1 45.1 %copy-start.23 = (f32[512]{0:T(512)S(1)}, f32[512]{0:T(512)}, u32[]{:S(2)}) copy-start(f32[512]{0:T(512)} %param.18) | copy-start | bytes 6148
  189.9 1.1 copy-start.3
  191.0 1.1 copy-start.6
  192.1 1.1 copy-start.5
  193.3 1.1 copy-start.4
  194.4 1.1 copy-start.2
  196.7 1.5 copy-start.1
  196.7 0.7 copy-start.24
Sparse Core Ops, SparseCore 0:
  8.9 174.3 all-gather.1
where the time goes:
time: 206 us; the launch traced here: 205 us
  waiting for transfers between devices  82 us (40%)
  blocking collectives  43.8 us (21%)
  local copies, waits for them, and re-layouts  25 us (12%)
  starting transfers between devices  17.9 us (9%)
  between operations  14 us (7%)
  other arithmetic  13.3 us (6%)
  matrix products  9.1 us (4%)
    all_gather x1, waiting for transfers between devices, per_device(): lax.all_gather(conv2_weight, 'width', axis=3, tiled=True)  62.3 us
    psum x1, blocking collectives, per_device(): sums, squares = lax.psum((sums, squares), ('tm', 'height', 'width'))  43.8 us
    concatenate x14, other arithmetic, convolve(): jnp.concatenate([padded[frame_tap:frame_tap + frames, row_tap:row_tap + r...  10.1 us
    dot_general x18, matrix products, convolve(): jnp.dot(window.reshape(-1, 3 * channels), taps, preferred_element_type=jn...  8.74 us
    ppermute x2, waiting for transfers between devices, with_halo(): after = lax.ppermute(leading, axis, down)  8.6 us
    unnamed x58, local copies, waits for them, and re-layouts  6.88 us
    slice x2, local copies, waits for them, and re-layouts, convolve(): taps = weight[:, row_tap, col_tap].reshape(3 * channels, outputs)  6.68 us
    all_to_all x1, waiting for transfers between devices, per_device(): lax.all_to_all(sectioned, 'height', split_axis=1, concat_axis=0, tiled=True)  5.58 us
  transfers between devices with their start and end apart: 8, of which 8 were waited for; matrix products, arithmetic and copies ran while one was open for 15% of the time, Pallas kernels for 0%

commit v1 on v0

v1 whole, which is shorter than its diff:
```python
import jax
import jax.numpy as jnp
from jax import lax
from jax.experimental import pallas as pl
from jax.experimental.pallas import tpu as pltpu
from jax.sharding import PartitionSpec as P

GROUPS = 32
FRAMES = 4
ROWS = 8
COLS = 8
AXES = ("tm", "height", "width")
bf16 = jnp.bfloat16
f32 = jnp.float32


def project_kernel(tok_ref, shift_ref, scale_ref, weight_ref, bias_ref, out_ref):
    values = tok_ref[...].astype(f32)
    center = jnp.mean(values, axis=-1, keepdims=True)
    values = values - center
    spread = jnp.mean(values * values, axis=-1, keepdims=True)
    normed = (values * lax.rsqrt(spread + 1e-06) * (1.0 + scale_ref[...]) + shift_ref[...]).astype(bf16)
    patches = lax.dot_general(normed, weight_ref[...], (((1,), (1,)), ((), ())), preferred_element_type=f32)
    patches = (patches + bias_ref[...]).astype(bf16)
    size = patches.shape[1]
    lat = size // 4
    source = lax.broadcasted_iota(jnp.int32, (size, size), 0)
    target = lax.broadcasted_iota(jnp.int32, (size, size), 1)
    wanted = 4 * (target % lat) + target // lat
    order = jnp.where(source == wanted, 1.0, 0.0).astype(bf16)
    patches = jnp.dot(patches, order, preferred_element_type=f32)
    half = patches.shape[0] // 2
    out_ref[...] = jnp.concatenate([patches[:half], patches[half:]], axis=1).astype(bf16)


def project(tokens, shift_mod, scale_mod, proj_weight, proj_bias):
    count, features = tokens.shape[0], proj_weight.shape[0]
    return pl.pallas_call(
        project_kernel,
        out_shape=jax.ShapeDtypeStruct((count // 2, 2 * features), bf16),
        name="project",
    )(tokens, shift_mod[None], scale_mod[None], proj_weight, proj_bias[None])


def decode_kernel(
    pos_ref,
    latent_ref,
    w1_ref,
    b1_ref,
    gain_ref,
    nbias_ref,
    w2_hbm,
    own_ref,
    other_ref,
    window,
    banded,
    hidden,
    field,
    cols,
    total,
    w2_ref,
    sem,
    *,
    NT,
    HP,
    WP,
    FT,
    TH,
    TW,
):
    C = w1_ref.shape[4]
    LAT = w1_ref.shape[3]
    C2 = w2_ref.shape[4]
    W = 2 * WP
    copy = pltpu.make_async_copy(w2_hbm, w2_ref, sem)
    copy.start()
    tm, height, width = pos_ref[0], pos_ref[1], pos_ref[2]

    for a in range(3):
        for v in range(2):
            for z in range(2):
                for i in range(2):
                    for j in range(2):
                        row = i if v == 0 else (-1 if i == 1 else 2)
                        col = j if z == 0 else (-1 if j == 1 else 2)
                        start = a * 16 * LAT + (((v * 2 + z) * 2 + i) * 2 + j) * LAT
                        for oi in range(2):
                            for oj in range(2):
                                b, e = row - oi + 1, col - oj + 1
                                at = (oi * 2 + oj) * C
                                if 0 <= b < 3 and 0 <= e < 3:
                                    banded[start : start + LAT, at : at + C] = w1_ref[a, b, e]
                                else:
                                    banded[start : start + LAT, at : at + C] = jnp.zeros((LAT, C), bf16)

    rows = latent_ref.shape[1]
    PR = rows // WP
    chunks = HP * WP // (2 * rows)
    frame_rows = HP * WP
    LN = 8 * LAT
    window[0 : 2 * frame_rows, :] = jnp.zeros((2 * frame_rows, 2 * LN), bf16)
    lane = lax.broadcasted_iota(jnp.int32, (rows, LN), 1)
    q = lax.broadcasted_iota(jnp.int32, (rows, LN), 0) % WP
    j_one = (lane // LAT) % 2 == 1
    low = lane < LN // 2
    keep = (j_one & (q > 0)) | (jnp.logical_not(j_one) & (q < WP - 1))
    i_one = (lax.broadcasted_iota(jnp.int32, (frame_rows, LN), 1) // (2 * LAT)) % 2 == 1

    def frame_body(t, carry):
        pieces = []
        for k in range(chunks):
            x = latent_ref[t * chunks + k].astype(f32)
            z = jnp.where(j_one, pltpu.roll(x, 1, 0), pltpu.roll(x, rows - 1, 0))
            z = jnp.where(keep, z, 0.0)
            zr = pltpu.roll(z, LN // 2, 1)
            xr = pltpu.roll(x, LN // 2, 1)
            pieces.append(jnp.where(low, x, zr))
            pieces.append(jnp.where(low, xr, z))
        y = jnp.concatenate(pieces, axis=0)
        zero = jnp.zeros((WP, LN), f32)
        above = jnp.concatenate([zero, y[:-WP]], axis=0)
        below = jnp.concatenate([y[WP:], zero], axis=0)
        v = jnp.where(i_one, above, below)
        base = pl.multiple_of((t + 2) * frame_rows, frame_rows)
        window[pl.ds(base, frame_rows), 0:LN] = y.astype(bf16)
        window[pl.ds(base, frame_rows), LN : 2 * LN] = v.astype(bf16)
        return carry

    lax.fori_loop(0, NT, frame_body, 0)

    FC = 4
    M = FC * frame_rows
    bias = b1_ref[...]
    sums = []
    squares = []
    hidden[:, 0:2, :, :, :] = jnp.zeros((4, 2, HP, WP, C), f32)
    for n in range(4):

        def chunk_body(g, carry, n=n):
            s, sq = carry
            at = pl.multiple_of(g * M, M)
            taps = jnp.concatenate(
                [window[pl.ds(pl.multiple_of(at + a * frame_rows, frame_rows), M), :] for a in range(3)], axis=1
            )
            h = jnp.dot(taps, banded[:, n * C : (n + 1) * C], preferred_element_type=f32) + bias
            hidden[n, pl.ds(g * FC + 2, FC)] = h.reshape(FC, HP, WP, C)
            h8 = h.reshape(M // 8, 8, C)
            return s + jnp.sum(h8, axis=0), sq + jnp.sum(h8 * h8, axis=0)

        s, sq = lax.fori_loop(0, NT // FC, chunk_body, (jnp.zeros((8, C), f32), jnp.zeros((8, C), f32)))
        sums.append(s)
        squares.append(sq)
    s = sums[0] + sums[1] + sums[2] + sums[3]
    sq = squares[0] + squares[1] + squares[2] + squares[3]
    s = jnp.broadcast_to(jnp.sum(s, axis=0, keepdims=True), (8, C))
    sq = jnp.broadcast_to(jnp.sum(sq, axis=0, keepdims=True), (8, C))
    size = gain_ref.shape[1] * lax.axis_size("width") // GROUPS
    member = jnp.where(
        lax.broadcasted_iota(jnp.int32, (C, C), 0) // size == lax.broadcasted_iota(jnp.int32, (C, C), 1) // size, 1.0, 0.0
    )
    count = NT * HP * WP * 4 * size
    gmean = jnp.dot(s, member, preferred_element_type=f32, precision=lax.Precision.HIGHEST)[0:1] / count
    second = jnp.dot(sq, member, preferred_element_type=f32, precision=lax.Precision.HIGHEST)[0:1] / count
    gvar = second - gmean * gmean
    inverse = lax.rsqrt(gvar + 1e-06)
    gain = gain_ref[...]
    nbias = nbias_ref[...]

    R = TH + 2
    PADW = W + 16
    edge = jnp.zeros(field.shape[:2] + (1, 128), f32)
    field[:, :, 7:8, :] = edge
    field[:, :, 8 + W : 9 + W, :] = edge
    first = height * (TH // 2) - 1

    def act_body(t, carry):
        frame = tm * FT + t
        for pp in range(TH // 2 + 2):
            prow = first + pp
            source = jnp.clip(prow, 0, HP - 1)
            inside = (frame >= 2) & (prow >= 0) & (prow < HP)
            for oi in range(2):
                row = 2 * pp + oi - 1
                if row < 0 or row >= R:
                    continue
                for oj in range(2):
                    h = hidden[oi * 2 + oj, frame, source].astype(bf16).astype(f32)
                    scaled = (h - gmean) * inverse * gain + nbias
                    act = scaled / (1.0 + jnp.exp(-scaled))
                    act = jnp.where(inside, act, 0.0)
                    for plane in range(field.shape[0]):
                        part = act[:, plane * 128 : (plane + 1) * 128]
                        if C < 128:
                            part = jnp.concatenate([part, jnp.zeros((WP, 128 - C), f32)], axis=1)
                        field[plane, t * R + row, pl.ds(8 + oj, WP, stride=2), :] = part
        return carry

    lax.fori_loop(0, FT + 2, act_body, 0)

    def cols_body(t, carry):
        for r in range(R):
            for e in range(3):
                for plane in range(field.shape[0]):
                    lanes = min(C, 128)
                    at = e * C + plane * 128
                    part = field[plane, t * R + r, 7 + e : 7 + e + W, :]
                    cols[t, r, :, at : at + lanes] = part[:, :lanes].astype(bf16)
        return carry

    lax.fori_loop(0, FT + 2, cols_body, 0)

    copy.wait()
    M2 = FT * TH * W
    for a in range(3):
        for b in range(3):
            taps = cols[a : a + FT, b : b + TH].reshape(M2, 3 * C)
            part = jnp.dot(taps, w2_ref[a, b].reshape(3 * C, C2), preferred_element_type=f32)
            if a == 0 and b == 0:
                total[...] = part
            else:
                total[...] += part

    tiles = W // TW
    result = total[...].reshape(FT * TH, tiles, TW, C2)
    if tiles == 2:
        mine = width == 0
        own_ref[...] = jnp.where(mine, result[:, 0], result[:, 1])
        other_ref[0] = jnp.where(mine, result[:, 1], result[:, 0]).astype(bf16)
    else:
        for k in range(tiles):

            @pl.when(width == k)
            def _(k=k):
                own_ref[...] = result[:, k]
                for step in range(1, tiles):
                    other_ref[step - 1] = result[:, (k + step) % tiles].astype(bf16)


def per_device(
    tokens,
    shift_mod,
    scale_mod,
    proj_weight,
    proj_bias,
    conv1_weight,
    conv1_bias,
    norm_gain,
    norm_bias,
    conv2_weight,
    conv2_bias,
    *,
    clip,
):
    width_count = lax.axis_size("width")
    height_count = lax.axis_size("height")
    time_count = lax.axis_size("tm")
    devices = width_count * height_count * time_count
    NT, NH, NW = clip
    FT, TH, TW = FRAMES, ROWS, COLS
    C2 = conv2_weight.shape[4]
    HP, WP = NH // 2, NW // 2
    C = conv2_weight.shape[3]
    LAT = conv1_weight.shape[3]

    chunk = project(tokens, shift_mod, scale_mod, proj_weight, proj_bias)
    spread = jnp.broadcast_to(chunk[None], (devices,) + chunk.shape)
    latent = lax.all_to_all(spread, AXES, 0, 0, tiled=True)

    width = lax.axis_index("width")
    position = jnp.stack([lax.axis_index("tm"), lax.axis_index("height"), width]).astype(jnp.int32)
    take = lambda x, axis: lax.dynamic_slice_in_dim(x, width * C, C, axis)
    smem = pl.BlockSpec(memory_space=pltpu.SMEM)
    vmem = pl.BlockSpec(memory_space=pltpu.VMEM)
    own, other = pl.pallas_call(
        lambda *refs: decode_kernel(*refs, NT=NT, HP=HP, WP=WP, FT=FT, TH=TH, TW=TW),
        out_shape=(
            jax.ShapeDtypeStruct((FT * TH, TW, C2), f32),
            jax.ShapeDtypeStruct((width_count - 1, FT * TH, TW, C2), bf16),
        ),
        in_specs=[smem, vmem, vmem, vmem, vmem, vmem, pl.BlockSpec(memory_space=pl.ANY)],
        out_specs=(vmem, vmem),
        scratch_shapes=[
            pltpu.VMEM(((NT + 2) * HP * WP, 16 * LAT), bf16),
            pltpu.VMEM((48 * LAT, 4 * C), bf16),
            pltpu.VMEM((4, NT + 2, HP, WP, C), f32),
            pltpu.VMEM((pl.cdiv(C, 128), (FT + 2) * (TH + 2), NW + 16, 128), f32),
            pltpu.VMEM((FT + 2, TH + 2, NW, 3 * C), bf16),
            pltpu.VMEM((FT * TH * NW, C2), f32),
            pltpu.VMEM(conv2_weight.shape, bf16),
            pltpu.SemaphoreType.DMA,
        ],
        compiler_params=pltpu.CompilerParams(vmem_limit_bytes=60 * 1024 * 1024),
        name="decode",
    )(
        position,
        latent,
        take(conv1_weight, 4),
        take(conv1_bias, 0)[None],
        take(norm_gain, 0)[None],
        take(norm_bias, 0)[None],
        conv2_weight,
    )
    result = own + conv2_bias
    for step in range(1, width_count):
        moved = lax.ppermute(other[step - 1], "width", [(k, (k + step) % width_count) for k in range(width_count)])
        result = result + moved.astype(f32)
    return result.reshape(FT, TH, TW, C2).astype(bf16)


def solution(mesh):
    placed = (
        P(AXES, None),
        P(),
        P(),
        P(),
        P(),
        P(),
        P(),
        P(),
        P(),
        P(None, None, None, "width", None),
        P(),
    )

    shape = (FRAMES * mesh.shape["tm"], ROWS * mesh.shape["height"], COLS * mesh.shape["width"])
    return jax.shard_map(
        lambda *args: per_device(*args, clip=shape),
        mesh=mesh,
        in_specs=placed,
        out_specs=P("tm", "height", "width", None),
        check_vma=False,
    )
```

time: 206 us -> 47.8 us (0.23)
  waiting for transfers between devices: 82 us -> 12.2 us
  blocking collectives: 43.8 us -> 0 us
  local copies, waits for them, and re-layouts: 25 us -> 6.84 us
  Pallas kernels: 0 us -> 17.2 us
  between operations: 14 us -> 0.03 us
  other arithmetic: 13.3 us -> 2.47 us
  starting transfers between devices: 17.9 us -> 8.59 us
  matrix products: 9.1 us -> 0 us
    all_gather x1 -> x0, waiting for transfers between devices: 62.3 us -> none  [per_device(): lax.all_gather(conv2_weight, 'width', axis=3, tiled=True)]
    psum x1 -> x0, blocking collectives: 43.8 us -> none  [per_device(): sums, squares = lax.psum((sums, squares), ('tm', 'height', 'width'))]
    pallas_call x0 -> x2, Pallas kernels: none -> 17.2 us  [the longest x1 14.7 us: per_device(): pl.pallas_call(lambda *refs: decode_kernel(*refs, NT=NT, HP=HP, WP=WP, FT...]
    concatenate x16 -> x0, other arithmetic: 10.4 us -> none  [the longest x14 10.1 us: convolve(): jnp.concatenate([padded[frame_tap:frame_tap + frames, row_tap:row_tap + r...]
    slice x7 -> x0, local copies, waits for them, and re-layouts: 10.3 us -> none  [the longest x2 6.68 us: convolve(): taps = weight[:, row_tap, col_tap].reshape(3 * channels, outputs)]
    dot_general x19 -> x0, matrix products: 9.1 us -> none  [the longest x18 8.74 us: convolve(): jnp.dot(window.reshape(-1, 3 * channels), taps, preferred_element_type=jn...]
    ppermute x5 -> x1, starting transfers between devices: 8.32 us -> 1.26 us  [per_device(): lax.ppermute(other[step - 1], 'width', [(k, (k + step) % width_count) for...]
    reshape x12 -> x0, local copies, waits for them, and re-layouts: 6.66 us -> none  [the longest x9 5.27 us: convolve(): window.reshape(-1, 3 * channels)]
  transfers between devices with their start and end apart: 8 -> 2, of which waited for: 8 -> 2; matrix products, arithmetic and copies ran while one was open for 15% -> 11% of each run, Pallas kernels for 0% -> 0%
where the time goes in v1:
time: 47.8 us; the launch traced here: 47.4 us
  Pallas kernels  17.2 us (36%)
  waiting for transfers between devices  12.2 us (26%)
  starting transfers between devices  8.59 us (18%)
  local copies, waits for them, and re-layouts  6.84 us (14%)
  other arithmetic  2.47 us (5%)
    pallas_call x1, Pallas kernels, per_device(): pl.pallas_call(lambda *refs: decode_kernel(*refs, NT=NT, HP=HP, WP=WP, FT...  14.7 us
    all_to_all x1, starting transfers between devices, per_device(): latent = lax.all_to_all(spread, AXES, 0, 0, tiled=True)  7.32 us
    ppermute x1, waiting for transfers between devices, per_device(): lax.ppermute(other[step - 1], 'width', [(k, (k + step) % width_count) for...  7.15 us
    all_to_all x1, waiting for transfers between devices, per_device(): latent = lax.all_to_all(spread, AXES, 0, 0, tiled=True)  5.08 us
    dynamic_slice x4, local copies, waits for them, and re-layouts, per_device(): take = lambda x, axis: lax.dynamic_slice_in_dim(x, width * C, C, axis)  4.7 us
    pallas_call x1, Pallas kernels, project(): pl.pallas_call(project_kernel, out_shape=jax.ShapeDtypeStruct((count // 2...  2.53 us
    convert_element_type x1, other arithmetic, per_device(): return result.reshape(FT, TH, TW, C2).astype(bf16)  1.83 us
    broadcast_in_dim x1, local copies, waits for them, and re-layouts, per_device(): spread = jnp.broadcast_to(chunk[None], (devices,) + chunk.shape)  1.43 us
  transfers between devices with their start and end apart: 2, of which 2 were waited for; matrix products, arithmetic and copies ran while one was open for 11% of the time, Pallas kernels for 0%

profile of v1, /device:TPU:0, one launch (start us, length us, event | category | flops | bytes accessed | tf_op | source)
XLA Modules:
  0.0 47.4 jit_solution(8828832863387468855)
XLA Ops:
  0.0 0.0 copy-start
  0.0 0.0 copy-start.2
  0.0 2.5 %project.1 = bf16[32,128]{1,0:T(8,128)(2,1)} custom-call(bf16[64,3072]{1,0:T(8,128)(2,1)} %tok_ref.1, f32[1,3072]{1,0:T(1,128)} %bitcast.11, f32[1,3072]{1,0:T(1,128)} %bitcast.12, bf16[64,3072]{1,0:T(8,128)(2,1)} %weight_ref.1, f32[1,64]{1,0:T(1,128)} %bitcast.16), custom_call_target="tpu_custom_call" | custom-call | tf_op jit(solution)/shard_map/project/pallas_call | solution.py:38
  2.5 1.4 %broadcast_in_dim.28 = bf16[32,32,128]{2,1,0:T(8,128)(2,1)} broadcast(bf16[32,128]{1,0:T(8,128)(2,1)} %project.1), dimensions={1,2} | broadcast | bytes 270336 | tf_op jit(solution)/shard_map/broadcast_in_dim | solution.py:266
  4.0 7.3 %all-to-all-start = ((bf16[32,32,128]{2,1,0:T(8,128)(2,1)}), bf16[32,32,128]{2,1,0:T(8,128)(2,1)S(1)}, u32[]{:S(2)}, u32[]{:S(2)}) async-start(bf16[32,32,128]{2,1,0:T(8,128)(2,1)} %broadcast_in_dim.28), calls=%async_computation | async-start | bytes 524288 | tf_op jit(solution)/shard_map/all_to_all | solution.py:267
  11.3 1.3 %dynamic_slice.13 = f32[256]{0:T(256)} dynamic-slice(f32[512]{0:T(512)} %param.17, s32[]{:T(128)S(6)} %select_n.2), dynamic_slice_sizes={256} | dynamic-slice | bytes 2052 | tf_op jit(solution)/shard_map/dynamic_slice | solution.py:271
  12.7 1.3 %dynamic_slice.14 = f32[256]{0:T(256)} dynamic-slice(f32[512]{0:T(512)} %param.18, s32[]{:T(128)S(6)} %select_n.2), dynamic_slice_sizes={256} | dynamic-slice | bytes 2052 | tf_op jit(solution)/shard_map/dynamic_slice | solution.py:271
  14.0 1.3 %dynamic_slice.15 = f32[256]{0:T(256)} dynamic-slice(f32[512]{0:T(512)} %param.19, s32[]{:T(128)S(6)} %select_n.2), dynamic_slice_sizes={256} | dynamic-slice | bytes 2052 | tf_op jit(solution)/shard_map/dynamic_slice | solution.py:271
  15.3 0.6 %pad_add_fusion.refs_0_ = s32[3]{0:T(128)} fusion(s32[1]{0:T(128)} %bitcast.2, s32[1]{0:T(128)} %bitcast.1, s32[1]{0:T(128)} %bitcast), kind=kLoop, calls=%fused_computation.1 | loop fusion | flops 6 | bytes 24 | tf_op jit(solution)/shard_map/stack | solution.py:270
  16.0 0.0 copy-done
  16.0 0.7 %constant_dynamic-slice_fusion.refs_2_ = bf16[3,3,3,16,256]{4,3,2,1,0:T(8,128)(2,1)} fusion(bf16[3,3,3,16,512]{4,3,2,1,0:T(8,128)(2,1)S(1)} %copy-done, s32[]{:T(128)S(6)} %select_n.2), kind=kLoop, calls=%fused_computation.2 | loop fusion | bytes 442372 | tf_op jit(solution)/shard_map/dynamic_slice | solution.py:271
  16.7 5.1 %all-to-all-done.refs_1_ = bf16[32,32,128]{2,1,0:T(8,128)(2,1)S(1)} async-done(((bf16[32,32,128]{2,1,0:T(8,128)(2,1)}), bf16[32,32,128]{2,1,0:T(8,128)(2,1)S(1)}, u32[]{:S(2)}, u32[]{:S(2)}) %all-to-all-start) | async-done | bytes 262176 | tf_op jit(solution)/shard_map/all_to_all | solution.py:267
  21.7 0.0 copy-start.1
  21.7 0.7 %copy-done.1 = bf16[32,32,128]{2,1,0:T(8,128)(2,1)} copy-done((bf16[32,32,128]{2,1,0:T(8,128)(2,1)}, bf16[32,32,128]{2,1,0:T(8,128)(2,1)S(1)}, u32[]{:S(2)}) %copy-start.1) | copy-done | bytes 262168
  22.5 14.7 %decode.1 = (f32[32,8,512]{2,1,0:T(8,128)}, bf16[1,32,8,512]{3,2,1,0:T(8,128)(2,1)}) custom-call(s32[3]{0:T(128)} %pad_add_fusion.refs_0_, bf16[32,32,128]{2,1,0:T(8,128)(2,1)} %copy-done.1, bf16[3,3,3,16,256]{4,3,2,1,0:T(8,128)(2,1)} %constant_dynamic-slice_fusion.refs_2_, f32[1,256]{1,0:T(1,128)} %bitcast.13, f32[1,256]{1,0:T(1,128)} %bitcast.14, ...), custom_call_target="tpu_custom_call" | custom-call | tf_op jit(solution)/shard_map/decode/pallas_call | solution.py:274
  37.2 1.3 %collective-permute-start = (bf16[32,8,512]{2,1,0:T(8,128)(2,1)}, bf16[32,8,512]{2,1,0:T(8,128)(2,1)S(1)}, u32[]{:S(2)}, u32[]{:S(2)}) collective-permute-start(bf16[32,8,512]{2,1,0:T(8,128)(2,1)} %bitcast.17), channel_id=1, source_target_pairs={{0,1},{1,0},{2,3},{3,2},{4,5},{5,4},{6,7},{7,6},{8,9},{9,8},{10,11... | collective-permute-start | bytes 786440 | tf_op jit(solution)/shard_map/ppermute | solution.py:305
  38.4 7.2 %collective-permute-done = bf16[32,8,512]{2,1,0:T(8,128)(2,1)S(1)} collective-permute-done((bf16[32,8,512]{2,1,0:T(8,128)(2,1)}, bf16[32,8,512]{2,1,0:T(8,128)(2,1)S(1)}, u32[]{:S(2)}, u32[]{:S(2)}) %collective-permute-start) | collective-permute-done | bytes 262176 | tf_op jit(solution)/shard_map/ppermute | solution.py:305
  45.6 0.0 copy-done.2
  45.6 1.8 %add_convert_fusion = bf16[32,8,512]{2,1,0:T(8,128)(2,1)} fusion(bf16[32,8,512]{2,1,0:T(8,128)(2,1)S(1)} %collective-permute-done, f32[32,8,512]{2,1,0:T(8,128)} %get-tuple-element.7, f32[512]{0:T(512)S(1)} %copy-done.2), kind=kLoop, calls=%fused_computation | loop fusion | flops 524288 | bytes 1050624 | tf_op jit(solution)/shard_map/convert_element_type | solution.py:307
Async XLA Ops:
  0.0 16.0 %copy-start = (bf16[3,3,3,16,512]{4,3,2,1,0:T(8,128)(2,1)S(1)}, bf16[3,3,3,16,512]{4,3,2,1,0:T(8,128)(2,1)}, u32[]{:S(2)}) copy-start(bf16[3,3,3,16,512]{4,3,2,1,0:T(8,128)(2,1)} %param.16) | copy-start | bytes 1327108
  0.0 45.6 %copy-start.2 = (f32[512]{0:T(512)S(1)}, f32[512]{0:T(512)}, u32[]{:S(2)}) copy-start(f32[512]{0:T(512)} %param.21) | copy-start | bytes 6148
  4.0 17.8 %all-to-all-start = ((bf16[32,32,128]{2,1,0:T(8,128)(2,1)}), bf16[32,32,128]{2,1,0:T(8,128)(2,1)S(1)}, u32[]{:S(2)}, u32[]{:S(2)}) async-start(bf16[32,32,128]{2,1,0:T(8,128)(2,1)} %broadcast_in_dim.28), calls=%async_computation | async-start | bytes 524288 | tf_op jit(solution)/shard_map/all_to_all | solution.py:267
  21.7 0.7 %copy-start.1 = (bf16[32,32,128]{2,1,0:T(8,128)(2,1)}, bf16[32,32,128]{2,1,0:T(8,128)(2,1)S(1)}, u32[]{:S(2)}) copy-start(bf16[32,32,128]{2,1,0:T(8,128)(2,1)S(1)} %all-to-all-done.refs_1_) | copy-start | bytes 786436
  37.2 8.4 %collective-permute-start = (bf16[32,8,512]{2,1,0:T(8,128)(2,1)}, bf16[32,8,512]{2,1,0:T(8,128)(2,1)S(1)}, u32[]{:S(2)}, u32[]{:S(2)}) collective-permute-start(bf16[32,8,512]{2,1,0:T(8,128)(2,1)} %bitcast.17), channel_id=1, source_target_pairs={{0,1},{1,0},{2,3},{3,2},{4,5},{5,4},{6,7},{7,6},{8,9},{9,8},{10,11... | collective-permute-start | bytes 786440 | tf_op jit(solution)/shard_map/ppermute | solution.py:305

commit v2 on v1

--- a/solution.py
+++ b/solution.py
@@ -30,14 +30,15 @@
     order = jnp.where(source == wanted, 1.0, 0.0).astype(bf16)
     patches = jnp.dot(patches, order, preferred_element_type=f32)
     half = patches.shape[0] // 2
-    out_ref[...] = jnp.concatenate([patches[:half], patches[half:]], axis=1).astype(bf16)
-
-
-def project(tokens, shift_mod, scale_mod, proj_weight, proj_bias):
+    packed = jnp.concatenate([patches[:half], patches[half:]], axis=1).astype(bf16)
+    out_ref[...] = jnp.broadcast_to(packed[None], out_ref.shape)
+
+
+def project(tokens, shift_mod, scale_mod, proj_weight, proj_bias, copies):
     count, features = tokens.shape[0], proj_weight.shape[0]
     return pl.pallas_call(
         project_kernel,
-        out_shape=jax.ShapeDtypeStruct((count // 2, 2 * features), bf16),
+        out_shape=jax.ShapeDtypeStruct((copies, count // 2, 2 * features), bf16),
         name="project",
     )(tokens, shift_mod[None], scale_mod[None], proj_weight, proj_bias[None])
 
@@ -126,14 +127,14 @@
         window[pl.ds(base, frame_rows), LN : 2 * LN] = v.astype(bf16)
         return carry
 
-    lax.fori_loop(0, NT, frame_body, 0)
-
-    FC = 4
+    lax.fori_loop(0, NT, frame_body, 0, unroll=4)
+
+    FC = max(1, 2048 // frame_rows)
     M = FC * frame_rows
     bias = b1_ref[...]
     sums = []
     squares = []
-    hidden[:, 0:2, :, :, :] = jnp.zeros((4, 2, HP, WP, C), f32)
+    hidden[0:2] = jnp.zeros((2, HP, WP, 4 * C), f32)
     for n in range(4):
 
         def chunk_body(g, carry, n=n):
@@ -143,7 +144,7 @@
                 [window[pl.ds(pl.multiple_of(at + a * frame_rows, frame_rows), M), :] for a in range(3)], axis=1
             )
             h = jnp.dot(taps, banded[:, n * C : (n + 1) * C], preferred_element_type=f32) + bias
-            hidden[n, pl.ds(g * FC + 2, FC)] = h.reshape(FC, HP, WP, C)
+            hidden[pl.ds(g * FC + 2, FC), :, :, n * C : (n + 1) * C] = h.reshape(FC, HP, WP, C)
             h8 = h.reshape(M // 8, 8, C)
             return s + jnp.sum(h8, axis=0), sq + jnp.sum(h8 * h8, axis=0)
 
@@ -184,7 +185,8 @@
                 if row < 0 or row >= R:
                     continue
                 for oj in range(2):
-                    h = hidden[oi * 2 + oj, frame, source].astype(bf16).astype(f32)
+                    at = (oi * 2 + oj) * C
+                    h = hidden[frame, source, :, at : at + C].astype(bf16).astype(f32)
                     scaled = (h - gmean) * inverse * gain + nbias
                     act = scaled / (1.0 + jnp.exp(-scaled))
                     act = jnp.where(inside, act, 0.0)
@@ -262,9 +264,9 @@
     C = conv2_weight.shape[3]
     LAT = conv1_weight.shape[3]
 
-    chunk = project(tokens, shift_mod, scale_mod, proj_weight, proj_bias)
-    spread = jnp.broadcast_to(chunk[None], (devices,) + chunk.shape)
+    spread = project(tokens, shift_mod, scale_mod, proj_weight, proj_bias, devices)
     latent = lax.all_to_all(spread, AXES, 0, 0, tiled=True)
+    latent = pltpu.with_memory_space_constraint(latent, pltpu.VMEM)
 
     width = lax.axis_index("width")
     position = jnp.stack([lax.axis_index("tm"), lax.axis_index("height"), width]).astype(jnp.int32)
@@ -274,22 +276,22 @@
     own, other = pl.pallas_call(
         lambda *refs: decode_kernel(*refs, NT=NT, HP=HP, WP=WP, FT=FT, TH=TH, TW=TW),
         out_shape=(
-            jax.ShapeDtypeStruct((FT * TH, TW, C2), f32),
-            jax.ShapeDtypeStruct((width_count - 1, FT * TH, TW, C2), bf16),
+            pltpu.VMEM((FT * TH, TW, C2), f32),
+            pltpu.VMEM((width_count - 1, FT * TH, TW, C2), bf16),
         ),
         in_specs=[smem, vmem, vmem, vmem, vmem, vmem, pl.BlockSpec(memory_space=pl.ANY)],
         out_specs=(vmem, vmem),
         scratch_shapes=[
             pltpu.VMEM(((NT + 2) * HP * WP, 16 * LAT), bf16),
             pltpu.VMEM((48 * LAT, 4 * C), bf16),
-            pltpu.VMEM((4, NT + 2, HP, WP, C), f32),
+            pltpu.VMEM((NT + 2, HP, WP, 4 * C), f32),
             pltpu.VMEM((pl.cdiv(C, 128), (FT + 2) * (TH + 2), NW + 16, 128), f32),
             pltpu.VMEM((FT + 2, TH + 2, NW, 3 * C), bf16),
             pltpu.VMEM((FT * TH * NW, C2), f32),
             pltpu.VMEM(conv2_weight.shape, bf16),
             pltpu.SemaphoreType.DMA,
         ],
-        compiler_params=pltpu.CompilerParams(vmem_limit_bytes=60 * 1024 * 1024),
+        compiler_params=pltpu.CompilerParams(vmem_limit_bytes=44 * 1024 * 1024),
         name="decode",
     )(
         position,

time: 47.8 us -> 43.2 us (0.904)
  Pallas kernels: 17.2 us -> 13.1 us
  waiting for transfers between devices: 12.2 us -> 15 us
  other arithmetic: 2.47 us -> 0.86 us
  local copies, waits for them, and re-layouts: 6.84 us -> 5.3 us
    pallas_call x1, Pallas kernels: 14.7 us -> 10.5 us  [per_device(): pl.pallas_call(lambda *refs: decode_kernel(*refs, NT=NT, HP=HP, WP=WP, FT...]
    all_to_all x1, waiting for transfers between devices: 5.08 us -> 8.06 us  [per_device(): latent = lax.all_to_all(spread, AXES, 0, 0, tiled=True)]
    dynamic_slice x4, local copies, waits for them, and re-layouts: 4.7 us -> 2.28 us  [per_device(): take = lambda x, axis: lax.dynamic_slice_in_dim(x, width * C, C, axis)]
    unnamed x6, local copies, waits for them, and re-layouts: 0.71 us -> 3.02 us
    broadcast_in_dim x1 -> x0, local copies, waits for them, and re-layouts: 1.43 us -> none  [per_device(): spread = jnp.broadcast_to(chunk[None], (devices,) + chunk.shape)]
    convert_element_type x1, other arithmetic: 1.83 us -> 0.79 us  [per_device(): return result.reshape(FT, TH, TW, C2).astype(bf16)]
    another operation x1, other arithmetic: 0.65 us -> 0.08 us  [per_device(): jnp.stack([lax.axis_index('tm'), lax.axis_index('height'), width])]
  transfers between devices with their start and end apart: 2 -> 2, of which waited for: 2 -> 2; matrix products, arithmetic and copies ran while one was open for 11% -> 5% of each run, Pallas kernels for 0% -> 0%
where the time goes in v2:
time: 43.2 us; the launch traced here: 42.9 us
  waiting for transfers between devices  15 us (35%)
  Pallas kernels  13.1 us (30%)
  starting transfers between devices  8.59 us (20%)
  local copies, waits for them, and re-layouts  5.3 us (12%)
  other arithmetic  0.86 us (2%)
    pallas_call x1, Pallas kernels, per_device(): pl.pallas_call(lambda *refs: decode_kernel(*refs, NT=NT, HP=HP, WP=WP, FT...  10.5 us
    all_to_all x1, waiting for transfers between devices, per_device(): latent = lax.all_to_all(spread, AXES, 0, 0, tiled=True)  8.06 us
    all_to_all x1, starting transfers between devices, per_device(): latent = lax.all_to_all(spread, AXES, 0, 0, tiled=True)  7.32 us
    ppermute x1, waiting for transfers between devices, per_device(): lax.ppermute(other[step - 1], 'width', [(k, (k + step) % width_count) for...  6.94 us
    unnamed x6, local copies, waits for them, and re-layouts  3.02 us
    pallas_call x1, Pallas kernels, project(): pl.pallas_call(project_kernel, out_shape=jax.ShapeDtypeStruct((copies, co...  2.65 us
    dynamic_slice x4, local copies, waits for them, and re-layouts, per_device(): take = lambda x, axis: lax.dynamic_slice_in_dim(x, width * C, C, axis)  2.28 us
    ppermute x1, starting transfers between devices, per_device(): lax.ppermute(other[step - 1], 'width', [(k, (k + step) % width_count) for...  1.27 us
  transfers between devices with their start and end apart: 2, of which 2 were waited for; matrix products, arithmetic and copies ran while one was open for 5% of the time, Pallas kernels for 0%

profile of v2, /device:TPU:0, one launch (start us, length us, event | category | flops | bytes accessed | tf_op | source)
XLA Modules:
  0.0 42.9 jit_solution(1875710169532832495)
XLA Ops:
  0.0 0.0 copy-start
  0.0 0.0 copy-start.2
  0.0 2.7 %project.1 = bf16[32,32,128]{2,1,0:T(8,128)(2,1)} custom-call(bf16[64,3072]{1,0:T(8,128)(2,1)} %tok_ref.1, f32[1,3072]{1,0:T(1,128)} %bitcast.15, f32[1,3072]{1,0:T(1,128)} %bitcast.16, bf16[64,3072]{1,0:T(8,128)(2,1)} %weight_ref.1, f32[1,64]{1,0:T(1,128)} %bitcast.17), custom_call_target="tpu_custom_call" | custom-call | tf_op jit(solution)/shard_map/project/pallas_call | solution.py:39
  2.7 7.3 %all-to-all-start = ((bf16[32,32,128]{2,1,0:T(8,128)(2,1)}), bf16[32,32,128]{2,1,0:T(8,128)(2,1)S(1)}, u32[]{:S(2)}, u32[]{:S(2)}) async-start(bf16[32,32,128]{2,1,0:T(8,128)(2,1)} %project.1), calls=%async_computation | async-start | bytes 524288 | tf_op jit(solution)/shard_map/all_to_all | solution.py:268
  10.0 0.8 %dynamic_slice.13 = f32[256]{0:T(256)S(1)} dynamic-slice(f32[512]{0:T(512)} %param.17, s32[]{:T(128)S(6)} %select_n.2), dynamic_slice_sizes={256} | dynamic-slice | bytes 2052 | tf_op jit(solution)/shard_map/dynamic_slice | solution.py:273
  10.8 0.8 %dynamic_slice.14 = f32[256]{0:T(256)S(1)} dynamic-slice(f32[512]{0:T(512)} %param.18, s32[]{:T(128)S(6)} %select_n.2), dynamic_slice_sizes={256} | dynamic-slice | bytes 2052 | tf_op jit(solution)/shard_map/dynamic_slice | solution.py:273
  11.5 0.8 %dynamic_slice.15 = f32[256]{0:T(256)S(1)} dynamic-slice(f32[512]{0:T(512)} %param.19, s32[]{:T(128)S(6)} %select_n.2), dynamic_slice_sizes={256} | dynamic-slice | bytes 2052 | tf_op jit(solution)/shard_map/dynamic_slice | solution.py:273
  12.3 0.1 pad_add_fusion.refs_0_
  12.3 0.0 copy-done
  12.4 8.1 %all-to-all-done.refs_1_ = bf16[32,32,128]{2,1,0:T(8,128)(2,1)S(1)} async-done(((bf16[32,32,128]{2,1,0:T(8,128)(2,1)}), bf16[32,32,128]{2,1,0:T(8,128)(2,1)S(1)}, u32[]{:S(2)}, u32[]{:S(2)}) %all-to-all-start) | async-done | bytes 262176 | tf_op jit(solution)/shard_map/all_to_all | solution.py:268
  20.4 0.0 copy-start.1
  20.4 3.0 %copy-done.1 = bf16[3,3,3,256,512]{4,3,2,1,0:T(8,128)(2,1)S(1)} copy-done((bf16[3,3,3,256,512]{4,3,2,1,0:T(8,128)(2,1)S(1)}, bf16[3,3,3,256,512]{4,3,2,1,0:T(8,128)(2,1)}, u32[]{:S(2)}) %copy-start.1) | copy-done | bytes 7077912
  23.4 10.5 %decode.1 = (f32[32,8,512]{2,1,0:T(8,128)S(1)}, bf16[1,32,8,512]{3,2,1,0:T(8,128)(2,1)S(1)}) custom-call(s32[3]{0:T(128)S(1)} %pad_add_fusion.refs_0_, bf16[32,32,128]{2,1,0:T(8,128)(2,1)S(1)} %all-to-all-done.refs_1_, bf16[3,3,3,16,256]{4,3,2,1,0:T(8,128)(2,1)S(1)} %constant_dynamic-slice_fusion.refs_2_, f32[1,256]{1,0:T(1,128)S(1)} %bitcast.11, ...), custom_call_target="tpu_custom_call" | custom-call | tf_op jit(solution)/shard_map/decode/pallas_call | solution.py:276
  33.9 1.3 %collective-permute-start = (bf16[32,8,512]{2,1,0:T(8,128)(2,1)S(1)}, bf16[32,8,512]{2,1,0:T(8,128)(2,1)S(1)}, u32[]{:S(2)}, u32[]{:S(2)}) collective-permute-start(bf16[32,8,512]{2,1,0:T(8,128)(2,1)S(1)} %bitcast.14), channel_id=1, source_target_pairs={{0,1},{1,0},{2,3},{3,2},{4,5},{5,4},{6,7},{7,6},{8,9},{9,8},{10,11... | collective-permute-start | bytes 786440 | tf_op jit(solution)/shard_map/ppermute | solution.py:307
  35.2 6.9 %collective-permute-done = bf16[32,8,512]{2,1,0:T(8,128)(2,1)S(1)} collective-permute-done((bf16[32,8,512]{2,1,0:T(8,128)(2,1)S(1)}, bf16[32,8,512]{2,1,0:T(8,128)(2,1)S(1)}, u32[]{:S(2)}, u32[]{:S(2)}) %collective-permute-start) | collective-permute-done | bytes 262176 | tf_op jit(solution)/shard_map/ppermute | solution.py:307
  42.1 0.0 copy-done.2
  42.1 0.8 %add_convert_fusion = bf16[32,8,512]{2,1,0:T(8,128)(2,1)} fusion(bf16[32,8,512]{2,1,0:T(8,128)(2,1)S(1)} %collective-permute-done, f32[32,8,512]{2,1,0:T(8,128)S(1)} %get-tuple-element.7, f32[512]{0:T(512)S(1)} %copy-done.2), kind=kLoop, calls=%fused_computation | loop fusion | flops 524288 | bytes 1050624 | tf_op jit(solution)/shard_map/convert_element_type | solution.py:309
  (1 shorter events, 0.0 us)
Async XLA Ops:
  0.0 12.3 %copy-start = (bf16[3,3,3,16,512]{4,3,2,1,0:T(8,128)(2,1)S(1)}, bf16[3,3,3,16,512]{4,3,2,1,0:T(8,128)(2,1)}, u32[]{:S(2)}) copy-start(bf16[3,3,3,16,512]{4,3,2,1,0:T(8,128)(2,1)} %param.16) | copy-start | bytes 1327108
  0.0 42.1 %copy-start.2 = (f32[512]{0:T(512)S(1)}, f32[512]{0:T(512)}, u32[]{:S(2)}) copy-start(f32[512]{0:T(512)} %param.21) | copy-start | bytes 6148
  2.7 17.8 %all-to-all-start = ((bf16[32,32,128]{2,1,0:T(8,128)(2,1)}), bf16[32,32,128]{2,1,0:T(8,128)(2,1)S(1)}, u32[]{:S(2)}, u32[]{:S(2)}) async-start(bf16[32,32,128]{2,1,0:T(8,128)(2,1)} %project.1), calls=%async_computation | async-start | bytes 524288 | tf_op jit(solution)/shard_map/all_to_all | solution.py:268
  20.4 3.0 %copy-start.1 = (bf16[3,3,3,256,512]{4,3,2,1,0:T(8,128)(2,1)S(1)}, bf16[3,3,3,256,512]{4,3,2,1,0:T(8,128)(2,1)}, u32[]{:S(2)}) copy-start(bf16[3,3,3,256,512]{4,3,2,1,0:T(8,128)(2,1)} %refs_6_.1) | copy-start | bytes 21233668
  33.9 8.2 %collective-permute-start = (bf16[32,8,512]{2,1,0:T(8,128)(2,1)S(1)}, bf16[32,8,512]{2,1,0:T(8,128)(2,1)S(1)}, u32[]{:S(2)}, u32[]{:S(2)}) collective-permute-start(bf16[32,8,512]{2,1,0:T(8,128)(2,1)S(1)} %bitcast.14), channel_id=1, source_target_pairs={{0,1},{1,0},{2,3},{3,2},{4,5},{5,4},{6,7},{7,6},{8,9},{9,8},{10,11... | collective-permute-start | bytes 786440 | tf_op jit(solution)/shard_map/ppermute | solution.py:307

commit v3 on v2

--- a/solution.py
+++ b/solution.py
@@ -43,39 +43,11 @@
     )(tokens, shift_mod[None], scale_mod[None], proj_weight, proj_bias[None])
 
 
-def decode_kernel(
-    pos_ref,
-    latent_ref,
-    w1_ref,
-    b1_ref,
-    gain_ref,
-    nbias_ref,
-    w2_hbm,
-    own_ref,
-    other_ref,
-    window,
-    banded,
-    hidden,
-    field,
-    cols,
-    total,
-    w2_ref,
-    sem,
-    *,
-    NT,
-    HP,
-    WP,
-    FT,
-    TH,
-    TW,
-):
-    C = w1_ref.shape[4]
-    LAT = w1_ref.shape[3]
-    C2 = w2_ref.shape[4]
-    W = 2 * WP
-    copy = pltpu.make_async_copy(w2_hbm, w2_ref, sem)
-    copy.start()
-    tm, height, width = pos_ref[0], pos_ref[1], pos_ref[2]
+def prepare_kernel(w1_ref, b1_ref, gain_ref, nbias_ref, banded, affine):
+    LAT, C = w1_ref.shape[3:]
+    affine[0:1, :] = b1_ref[...]
+    affine[1:2, :] = gain_ref[...]
+    affine[2:3, :] = nbias_ref[...]
 
     for a in range(3):
         for v in range(2):
@@ -93,6 +65,73 @@
                                     banded[start : start + LAT, at : at + C] = w1_ref[a, b, e]
                                 else:
                                     banded[start : start + LAT, at : at + C] = jnp.zeros((LAT, C), bf16)
+
+
+def prepare(conv1_weight, conv1_bias, norm_gain, norm_bias):
+    LAT, C = conv1_weight.shape[3:]
+    vmem = pl.BlockSpec(memory_space=pltpu.VMEM)
+    return pl.pallas_call(
+        prepare_kernel,
+        out_shape=(pltpu.VMEM((48 * LAT, 4 * C), bf16), pltpu.VMEM((3, C), f32)),
+        in_specs=[vmem] * 4,
+        out_specs=(vmem, vmem),
+        compiler_params=pltpu.CompilerParams(vmem_limit_bytes=16 * 1024 * 1024),
+        name="prepare",
+    )(conv1_weight, conv1_bias[None], norm_gain[None], norm_bias[None])
+
+
+def tile_products(cols, w2_ref, tile, n2, TH):
+    C, C2 = w2_ref.shape[3:]
+    total = None
+    for a, first in enumerate((0, n2 + 1, 1)):
+        for b in range(3):
+            taps = cols[tile, first : first + n2, b : b + TH]
+            taps = taps.reshape(n2 * TH * taps.shape[2], 3 * C)
+            part = jnp.dot(taps, w2_ref[a, b].reshape(3 * C, C2), preferred_element_type=f32)
+            total = part if total is None else total + part
+    return total
+
+
+def store_tile(total, out, n2, TH, TW):
+    total = total.reshape(n2, TH, 2, TW, total.shape[-1])
+    for p in range(n2):
+        for k in range(2):
+            out[2 * p + k] = total[p, :, k].astype(out.dtype)
+
+
+def own_kernel(pos_ref, cols, w2_ref, own_ref):
+    FT, TH, TW, _ = own_ref.shape
+    total = tile_products(cols, w2_ref, pos_ref[2], FT // 2, TH)
+    store_tile(total, own_ref, FT // 2, TH, TW)
+
+
+def decode_kernel(
+    pos_ref,
+    latent_ref,
+    banded,
+    affine,
+    w2_hbm,
+    other_ref,
+    cols,
+    w2_ref,
+    window,
+    hidden,
+    field,
+    sem,
+    *,
+    NT,
+    HP,
+    WP,
+    FT,
+    TH,
+    TW,
+):
+    C = w2_ref.shape[3]
+    LAT = banded.shape[0] // 48
+    W = 2 * WP
+    tm, height, width = pos_ref[0], pos_ref[1], pos_ref[2]
+    copy = pltpu.make_async_copy(w2_hbm, w2_ref, sem)
+    copy.start()
 
     rows = latent_ref.shape[1]
     PR = rows // WP
@@ -131,7 +170,7 @@
 
     FC = max(1, 2048 // frame_rows)
     M = FC * frame_rows
-    bias = b1_ref[...]
+    bias = affine[0:1, :]
     sums = []
     squares = []
     hidden[0:2] = jnp.zeros((2, HP, WP, 4 * C), f32)
@@ -155,7 +194,7 @@
     sq = squares[0] + squares[1] + squares[2] + squares[3]
     s = jnp.broadcast_to(jnp.sum(s, axis=0, keepdims=True), (8, C))
     sq = jnp.broadcast_to(jnp.sum(sq, axis=0, keepdims=True), (8, C))
-    size = gain_ref.shape[1] * lax.axis_size("width") // GROUPS
+    size = C * lax.axis_size("width") // GROUPS
     member = jnp.where(
         lax.broadcasted_iota(jnp.int32, (C, C), 0) // size == lax.broadcasted_iota(jnp.int32, (C, C), 1) // size, 1.0, 0.0
     )
@@ -164,8 +203,8 @@
     second = jnp.dot(sq, member, preferred_element_type=f32, precision=lax.Precision.HIGHEST)[0:1] / count
     gvar = second - gmean * gmean
     inverse = lax.rsqrt(gvar + 1e-06)
-    gain = gain_ref[...]
-    nbias = nbias_ref[...]
+    gain = affine[1:2, :]
+    nbias = affine[2:3, :]
 
     R = TH + 2
     PADW = W + 16
@@ -199,43 +238,29 @@
 
     lax.fori_loop(0, FT + 2, act_body, 0)
 
-    def cols_body(t, carry):
+    n2 = FT // 2
+    tiles = W // TW
+
+    def pair_body(k, carry):
+        t = jnp.where(k <= n2, 2 * k, 2 * (k - n2) - 1)
         for r in range(R):
-            for e in range(3):
-                for plane in range(field.shape[0]):
-                    lanes = min(C, 128)
-                    at = e * C + plane * 128
-                    part = field[plane, t * R + r, 7 + e : 7 + e + W, :]
-                    cols[t, r, :, at : at + lanes] = part[:, :lanes].astype(bf16)
+            for tile in range(tiles):
+                for e in range(3):
+                    at = 7 + e + tile * TW
+                    for plane in range(field.shape[0]):
+                        lanes = min(C, 128)
+                        lane_at = e * C + plane * 128
+                        parts = [field[plane, (t + k2) * R + r, at : at + TW, :] for k2 in range(2)]
+                        part = jnp.concatenate(parts, axis=0).astype(bf16)
+                        cols[tile, k, r, :, lane_at : lane_at + lanes] = part[:, :lanes]
         return carry
 
-    lax.fori_loop(0, FT + 2, cols_body, 0)
+    lax.fori_loop(0, 2 * n2 + 1, pair_body, 0)
 
     copy.wait()
-    M2 = FT * TH * W
-    for a in range(3):
-        for b in range(3):
-            taps = cols[a : a + FT, b : b + TH].reshape(M2, 3 * C)
-            part = jnp.dot(taps, w2_ref[a, b].reshape(3 * C, C2), preferred_element_type=f32)
-            if a == 0 and b == 0:
-                total[...] = part
-            else:
-                total[...] += part
-
-    tiles = W // TW
-    result = total[...].reshape(FT * TH, tiles, TW, C2)
-    if tiles == 2:
-        mine = width == 0
-        own_ref[...] = jnp.where(mine, result[:, 0], result[:, 1])
-        other_ref[0] = jnp.where(mine, result[:, 1], result[:, 0]).astype(bf16)
-    else:
-        for k in range(tiles):
-
-            @pl.when(width == k)
-            def _(k=k):
-                own_ref[...] = result[:, k]
-                for step in range(1, tiles):
-                    other_ref[step - 1] = result[:, (k + step) % tiles].astype(bf16)
+    for step in range(1, tiles):
+        tile = lax.rem(width + step, tiles)
+        store_tile(tile_products(cols, w2_ref, tile, n2, TH), other_ref.at[step - 1], n2, TH, TW)
 
 
 def per_device(
@@ -273,40 +298,53 @@
     take = lambda x, axis: lax.dynamic_slice_in_dim(x, width * C, C, axis)
     smem = pl.BlockSpec(memory_space=pltpu.SMEM)
     vmem = pl.BlockSpec(memory_space=pltpu.VMEM)
-    own, other = pl.pallas_call(
+    resident = lambda x: pltpu.with_memory_space_constraint(x, pltpu.VMEM)
+    conv2_weight = pltpu.with_memory_space_constraint(conv2_weight, pltpu.HBM)
+    banded, affine = prepare(
+        take(conv1_weight, 4), take(conv1_bias, 0), take(norm_gain, 0), take(norm_bias, 0)
+    )
+    banded, affine = resident(banded), resident(affine)
+    other, cols, w2 = pl.pallas_call(
         lambda *refs: decode_kernel(*refs, NT=NT, HP=HP, WP=WP, FT=FT, TH=TH, TW=TW),
         out_shape=(
-            pltpu.VMEM((FT * TH, TW, C2), f32),
-            pltpu.VMEM((width_count - 1, FT * TH, TW, C2), bf16),
+            pltpu.VMEM((width_count - 1, FT, TH, TW, C2), bf16),
+            pltpu.VMEM((width_count, FT + 1, TH + 2, 2 * TW, 3 * C), bf16),
+            pltpu.VMEM(conv2_weight.shape, bf16),
         ),
-        in_specs=[smem, vmem, vmem, vmem, vmem, vmem, pl.BlockSpec(memory_space=pl.ANY)],
-        out_specs=(vmem, vmem),
+        in_specs=[smem, vmem, vmem, vmem, pl.BlockSpec(memory_space=pl.ANY)],
+        out_specs=(vmem, vmem, vmem),
         scratch_shapes=[
             pltpu.VMEM(((NT + 2) * HP * WP, 16 * LAT), bf16),
-            pltpu.VMEM((48 * LAT, 4 * C), bf16),
             pltpu.VMEM((NT + 2, HP, WP, 4 * C), f32),
             pltpu.VMEM((pl.cdiv(C, 128), (FT + 2) * (TH + 2), NW + 16, 128), f32),
-            pltpu.VMEM((FT + 2, TH + 2, NW, 3 * C), bf16),
-            pltpu.VMEM((FT * TH * NW, C2), f32),
-            pltpu.VMEM(conv2_weight.shape, bf16),
             pltpu.SemaphoreType.DMA,
         ],
-        compiler_params=pltpu.CompilerParams(vmem_limit_bytes=44 * 1024 * 1024),
+        compiler_params=pltpu.CompilerParams(vmem_limit_bytes=40 * 1024 * 1024),
         name="decode",
     )(
         position,
         latent,
-        take(conv1_weight, 4),
-        take(conv1_bias, 0)[None],
-        take(norm_gain, 0)[None],
-        take(norm_bias, 0)[None],
+        banded,
+        affine,
         conv2_weight,
     )
-    result = own + conv2_bias
-    for step in range(1, width_count):
-        moved = lax.ppermute(other[step - 1], "width", [(k, (k + step) % width_count) for k in range(width_count)])
-        result = result + moved.astype(f32)
-    return result.reshape(FT, TH, TW, C2).astype(bf16)
+    cols, w2 = resident(cols), resident(w2)
+    moved = [
+        lax.ppermute(other[step - 1], "width", [(k, (k + step) % width_count) for k in range(width_count)])
+        for step in range(1, width_count)
+    ]
+    result = pl.pallas_call(
+        own_kernel,
+        out_shape=pltpu.VMEM((FT, TH, TW, C2), f32),
+        in_specs=[smem, vmem, vmem],
+        out_specs=vmem,
+        compiler_params=pltpu.CompilerParams(vmem_limit_bytes=8 * 1024 * 1024),
+        name="own",
+    )(position, cols, w2)
+    result = result + conv2_bias
+    for part in moved:
+        result = result + part.astype(f32)
+    return result.astype(bf16)
 
 
 def solution(mesh):

time: 43.2 us -> 38 us (0.88)
  local copies, waits for them, and re-layouts: 5.3 us -> 2.29 us
  waiting for transfers between devices: 15 us -> 12.4 us
    unnamed x6 -> x4, local copies, waits for them, and re-layouts: 3.02 us -> 0.01 us
    pallas_call x0 -> x2, Pallas kernels: none -> 2.62 us  [the longest x1 2.52 us: per_device(): pl.pallas_call(own_kernel, out_shape=pltpu.VMEM((FT, TH, TW, C2), f32), i...]
    ppermute x1, waiting for transfers between devices: 6.94 us -> 4.41 us  [per_device(): lax.ppermute(other[step - 1], 'width', [(k, (k + step) % width_count) for...]
    pallas_call x1, Pallas kernels: 10.5 us -> 8.24 us  [per_device(): pl.pallas_call(lambda *refs: decode_kernel(*refs, NT=NT, HP=HP, WP=WP, FT...]
  transfers between devices with their start and end apart: 2 -> 2, of which waited for: 2 -> 2; matrix products, arithmetic and copies ran while one was open for 5% -> 6% of each run, Pallas kernels for 0% -> 7%
where the time goes in v3:
time: 38 us; the launch traced here: 37.7 us
  Pallas kernels  13.5 us (36%)
  waiting for transfers between devices  12.4 us (33%)
  starting transfers between devices  8.6 us (23%)
  local copies, waits for them, and re-layouts  2.29 us (6%)
  other arithmetic  0.86 us (2%)
    pallas_call x1, Pallas kernels, per_device(): pl.pallas_call(lambda *refs: decode_kernel(*refs, NT=NT, HP=HP, WP=WP, FT...  8.24 us
    all_to_all x1, waiting for transfers between devices, per_device(): latent = lax.all_to_all(spread, AXES, 0, 0, tiled=True)  7.95 us
    all_to_all x1, starting transfers between devices, per_device(): latent = lax.all_to_all(spread, AXES, 0, 0, tiled=True)  7.33 us
    ppermute x1, waiting for transfers between devices, per_device(): lax.ppermute(other[step - 1], 'width', [(k, (k + step) % width_count) for...  4.41 us
    pallas_call x1, Pallas kernels, project(): pl.pallas_call(project_kernel, out_shape=jax.ShapeDtypeStruct((copies, co...  2.64 us
    pallas_call x1, Pallas kernels, per_device(): pl.pallas_call(own_kernel, out_shape=pltpu.VMEM((FT, TH, TW, C2), f32), i...  2.52 us
    dynamic_slice x4, local copies, waits for them, and re-layouts, per_device(): take = lambda x, axis: lax.dynamic_slice_in_dim(x, width * C, C, axis)  2.28 us
    ppermute x1, starting transfers between devices, per_device(): lax.ppermute(other[step - 1], 'width', [(k, (k + step) % width_count) for...  1.27 us
  transfers between devices with their start and end apart: 2, of which 2 were waited for; matrix products, arithmetic and copies ran while one was open for 6% of the time, Pallas kernels for 7%

profile of v3, /device:TPU:0, one launch (start us, length us, event | category | flops | bytes accessed | tf_op | source)
XLA Modules:
  0.0 37.7 jit_solution(18026393859918725259)
XLA Ops:
  0.0 0.0 copy-start
  0.0 2.6 %project.1 = bf16[32,32,128]{2,1,0:T(8,128)(2,1)} custom-call(bf16[64,3072]{1,0:T(8,128)(2,1)} %tok_ref.1, f32[1,3072]{1,0:T(1,128)} %bitcast.14, f32[1,3072]{1,0:T(1,128)} %bitcast.15, bf16[64,3072]{1,0:T(8,128)(2,1)} %weight_ref.1, f32[1,64]{1,0:T(1,128)} %bitcast.16), custom_call_target="tpu_custom_call" | custom-call | tf_op jit(solution)/shard_map/project/pallas_call | solution.py:39
  2.6 7.3 %all-to-all-start = ((bf16[32,32,128]{2,1,0:T(8,128)(2,1)}), bf16[32,32,128]{2,1,0:T(8,128)(2,1)S(1)}, u32[]{:S(2)}, u32[]{:S(2)}) async-start(bf16[32,32,128]{2,1,0:T(8,128)(2,1)} %project.1), calls=%async_computation | async-start | bytes 524288 | tf_op jit(solution)/shard_map/all_to_all | solution.py:293
  10.0 0.8 %dynamic_slice.13 = f32[256]{0:T(256)S(1)} dynamic-slice(f32[512]{0:T(512)} %param.17, s32[]{:T(128)S(6)} %select_n.2), dynamic_slice_sizes={256} | dynamic-slice | bytes 2052 | tf_op jit(solution)/shard_map/dynamic_slice | solution.py:298
  10.8 0.8 %dynamic_slice.14 = f32[256]{0:T(256)S(1)} dynamic-slice(f32[512]{0:T(512)} %param.18, s32[]{:T(128)S(6)} %select_n.2), dynamic_slice_sizes={256} | dynamic-slice | bytes 2052 | tf_op jit(solution)/shard_map/dynamic_slice | solution.py:298
  11.5 0.8 %dynamic_slice.15 = f32[256]{0:T(256)S(1)} dynamic-slice(f32[512]{0:T(512)} %param.19, s32[]{:T(128)S(6)} %select_n.2), dynamic_slice_sizes={256} | dynamic-slice | bytes 2052 | tf_op jit(solution)/shard_map/dynamic_slice | solution.py:298
  12.3 0.0 copy-done
  12.3 0.1 prepare.1
  12.4 0.1 pad_add_fusion.refs_0_.pos_ref
  12.5 7.9 %all-to-all-done.refs_1_ = bf16[32,32,128]{2,1,0:T(8,128)(2,1)S(1)} async-done(((bf16[32,32,128]{2,1,0:T(8,128)(2,1)}), bf16[32,32,128]{2,1,0:T(8,128)(2,1)S(1)}, u32[]{:S(2)}, u32[]{:S(2)}) %all-to-all-start) | async-done | bytes 262176 | tf_op jit(solution)/shard_map/all_to_all | solution.py:293
  20.4 8.2 %decode.1 = (bf16[1,4,8,8,512]{4,3,2,1,0:T(8,128)(2,1)S(1)}, bf16[2,5,10,16,768]{4,3,2,1,0:T(8,128)(2,1)S(1)}, bf16[3,3,3,256,512]{4,3,2,1,0:T(8,128)(2,1)S(1)}) custom-call(s32[3]{0:T(128)S(1)} %pad_add_fusion.refs_0_.pos_ref, bf16[32,32,128]{2,1,0:T(8,128)(2,1)S(1)} %all-to-all-done.refs_1_, bf16[768,1024]{1,0:T(8,128)(2,1)S(1)} %get-tuple-element.10.refs_2_, ...), custom_call_target="tpu_custom_call" | custom-call | tf_op jit(solution)/shard_map/decode/pallas_call | solution.py:307
  28.7 0.0 copy-start.1
  28.7 1.3 %collective-permute-start = (bf16[4,8,8,512]{3,2,1,0:T(8,128)(2,1)S(1)}, bf16[4,8,8,512]{3,2,1,0:T(8,128)(2,1)S(1)}, u32[]{:S(2)}, u32[]{:S(2)}) collective-permute-start(bf16[4,8,8,512]{3,2,1,0:T(8,128)(2,1)S(1)} %bitcast.13), channel_id=1, source_target_pairs={{0,1},{1,0},{2,3},{3,2},{4,5},{5,4},{6,7},{7,6},{8,9},{9,8},{10,11... | collective-permute-start | bytes 786440 | tf_op jit(solution)/shard_map/ppermute | solution.py:333
  30.0 2.5 %own.1 = f32[4,8,8,512]{3,2,1,0:T(8,128)S(1)} custom-call(s32[3]{0:T(128)S(1)} %pad_add_fusion.refs_0_.pos_ref, bf16[2,5,10,16,768]{4,3,2,1,0:T(8,128)(2,1)S(1)} %get-tuple-element.12.cols, bf16[3,3,3,256,512]{4,3,2,1,0:T(8,128)(2,1)S(1)} %get-tuple-element.13.w2_ref), custom_call_target="tpu_custom_call" | custom-call | tf_op jit(solution)/shard_map/own/pallas_call | solution.py:336
  32.5 4.4 %collective-permute-done = bf16[4,8,8,512]{3,2,1,0:T(8,128)(2,1)S(1)} collective-permute-done((bf16[4,8,8,512]{3,2,1,0:T(8,128)(2,1)S(1)}, bf16[4,8,8,512]{3,2,1,0:T(8,128)(2,1)S(1)}, u32[]{:S(2)}, u32[]{:S(2)}) %collective-permute-start) | collective-permute-done | bytes 262176 | tf_op jit(solution)/shard_map/ppermute | solution.py:333
  36.9 0.0 copy-done.1
  36.9 0.8 %add_convert_fusion = bf16[4,8,8,512]{3,2,1,0:T(8,128)(2,1)} fusion(bf16[4,8,8,512]{3,2,1,0:T(8,128)(2,1)S(1)} %collective-permute-done, f32[4,8,8,512]{3,2,1,0:T(8,128)S(1)} %own.1, f32[512]{0:T(512)S(1)} %copy-done.1), kind=kLoop, calls=%fused_computation | loop fusion | flops 524288 | bytes 1050624 | tf_op jit(solution)/shard_map/convert_element_type | solution.py:347
  (1 shorter events, 0.0 us)
Async XLA Ops:
  0.0 12.3 %copy-start = (bf16[3,3,3,16,512]{4,3,2,1,0:T(8,128)(2,1)S(1)}, bf16[3,3,3,16,512]{4,3,2,1,0:T(8,128)(2,1)}, u32[]{:S(2)}) copy-start(bf16[3,3,3,16,512]{4,3,2,1,0:T(8,128)(2,1)} %param.16) | copy-start | bytes 1327108
  2.6 17.8 %all-to-all-start = ((bf16[32,32,128]{2,1,0:T(8,128)(2,1)}), bf16[32,32,128]{2,1,0:T(8,128)(2,1)S(1)}, u32[]{:S(2)}, u32[]{:S(2)}) async-start(bf16[32,32,128]{2,1,0:T(8,128)(2,1)} %project.1), calls=%async_computation | async-start | bytes 524288 | tf_op jit(solution)/shard_map/all_to_all | solution.py:293
  28.7 8.2 %copy-start.1 = (f32[512]{0:T(512)S(1)}, f32[512]{0:T(512)}, u32[]{:S(2)}) copy-start(f32[512]{0:T(512)} %param.21) | copy-start | bytes 6148
  28.7 8.2 %collective-permute-start = (bf16[4,8,8,512]{3,2,1,0:T(8,128)(2,1)S(1)}, bf16[4,8,8,512]{3,2,1,0:T(8,128)(2,1)S(1)}, u32[]{:S(2)}, u32[]{:S(2)}) collective-permute-start(bf16[4,8,8,512]{3,2,1,0:T(8,128)(2,1)S(1)} %bitcast.13), channel_id=1, source_target_pairs={{0,1},{1,0},{2,3},{3,2},{4,5},{5,4},{6,7},{7,6},{8,9},{9,8},{10,11... | collective-permute-start | bytes 786440 | tf_op jit(solution)/shard_map/ppermute | solution.py:333

commit v4 on v3

--- a/solution.py
+++ b/solution.py
@@ -4,6 +4,7 @@
 from jax.experimental import pallas as pl
 from jax.experimental.pallas import tpu as pltpu
 from jax.sharding import PartitionSpec as P
+
 
 GROUPS = 32
 FRAMES = 4
@@ -36,11 +37,13 @@
 
 def project(tokens, shift_mod, scale_mod, proj_weight, proj_bias, copies):
     count, features = tokens.shape[0], proj_weight.shape[0]
+    operands = (tokens, shift_mod[None], scale_mod[None], proj_weight, proj_bias[None])
     return pl.pallas_call(
         project_kernel,
-        out_shape=jax.ShapeDtypeStruct((copies, count // 2, 2 * features), bf16),
+        out_shape=pltpu.VMEM((copies, count // 2, 2 * features), bf16),
+        compiler_params=pltpu.CompilerParams(vmem_limit_bytes=16 * 1024 * 1024),
         name="project",
-    )(tokens, shift_mod[None], scale_mod[None], proj_weight, proj_bias[None])
+    )(*[pltpu.with_memory_space_constraint(x, pltpu.HBM) for x in operands])
 
 
 def prepare_kernel(w1_ref, b1_ref, gain_ref, nbias_ref, banded, affine):
@@ -80,14 +83,14 @@
     )(conv1_weight, conv1_bias[None], norm_gain[None], norm_bias[None])
 
 
-def tile_products(cols, w2_ref, tile, n2, TH):
-    C, C2 = w2_ref.shape[3:]
+def tile_products(cols, w2_ref, tile, n2, TH, low, high):
+    C = w2_ref.shape[3]
     total = None
     for a, first in enumerate((0, n2 + 1, 1)):
         for b in range(3):
             taps = cols[tile, first : first + n2, b : b + TH]
             taps = taps.reshape(n2 * TH * taps.shape[2], 3 * C)
-            part = jnp.dot(taps, w2_ref[a, b].reshape(3 * C, C2), preferred_element_type=f32)
+            part = jnp.dot(taps, w2_ref[a, b, :, :, low:high].reshape(3 * C, high - low), preferred_element_type=f32)
             total = part if total is None else total + part
     return total
 
@@ -99,9 +102,21 @@
             out[2 * p + k] = total[p, :, k].astype(out.dtype)
 
 
+def send_tiles(cols, w2_ref, width, other_ref, low):
+    steps, FT, TH, TW, span = other_ref.shape
+    for step in range(steps):
+        tile = lax.rem(width + step + 1, steps + 1)
+        total = tile_products(cols, w2_ref, tile, FT // 2, TH, low, low + span)
+        store_tile(total, other_ref.at[step], FT // 2, TH, TW)
+
+
+def send_kernel(pos_ref, cols, w2_ref, other_ref, *, low):
+    send_tiles(cols, w2_ref, pos_ref[2], other_ref, low)
+
+
 def own_kernel(pos_ref, cols, w2_ref, own_ref):
     FT, TH, TW, _ = own_ref.shape
-    total = tile_products(cols, w2_ref, pos_ref[2], FT // 2, TH)
+    total = tile_products(cols, w2_ref, pos_ref[2], FT // 2, TH, 0, own_ref.shape[3])
     store_tile(total, own_ref, FT // 2, TH, TW)
 
 
@@ -134,7 +149,6 @@
     copy.start()
 
     rows = latent_ref.shape[1]
-    PR = rows // WP
     chunks = HP * WP // (2 * rows)
     frame_rows = HP * WP
     LN = 8 * LAT
@@ -203,11 +217,10 @@
     second = jnp.dot(sq, member, preferred_element_type=f32, precision=lax.Precision.HIGHEST)[0:1] / count
     gvar = second - gmean * gmean
     inverse = lax.rsqrt(gvar + 1e-06)
-    gain = affine[1:2, :]
-    nbias = affine[2:3, :]
+    slope = 0.5 * inverse * affine[1:2, :]
+    offset = 0.5 * affine[2:3, :]
 
     R = TH + 2
-    PADW = W + 16
     edge = jnp.zeros(field.shape[:2] + (1, 128), f32)
     field[:, :, 7:8, :] = edge
     field[:, :, 8 + W : 9 + W, :] = edge
@@ -226,8 +239,8 @@
                 for oj in range(2):
                     at = (oi * 2 + oj) * C
                     h = hidden[frame, source, :, at : at + C].astype(bf16).astype(f32)
-                    scaled = (h - gmean) * inverse * gain + nbias
-                    act = scaled / (1.0 + jnp.exp(-scaled))
+                    half = (h - gmean) * slope + offset
+                    act = half * jnp.tanh(half) + half
                     act = jnp.where(inside, act, 0.0)
                     for plane in range(field.shape[0]):
                         part = act[:, plane * 128 : (plane + 1) * 128]
@@ -258,12 +271,15 @@
     lax.fori_loop(0, 2 * n2 + 1, pair_body, 0)
 
     copy.wait()
-    for step in range(1, tiles):
-        tile = lax.rem(width + step, tiles)
-        store_tile(tile_products(cols, w2_ref, tile, n2, TH), other_ref.at[step - 1], n2, TH, TW)
-
-
-def per_device(
+
+    def once(k, carry):
+        send_tiles(cols, w2_ref, width + k, other_ref, 0)
+        return carry
+
+    lax.fori_loop(0, jnp.minimum(width + 1, 1), once, 0)
+
+
+def decode(
     tokens,
     shift_mod,
     scale_mod,
@@ -304,10 +320,12 @@
         take(conv1_weight, 4), take(conv1_bias, 0), take(norm_gain, 0), take(norm_bias, 0)
     )
     banded, affine = resident(banded), resident(affine)
+    span = C2 // 2
+    sent = pltpu.VMEM((width_count - 1, FT, TH, TW, span), bf16)
     other, cols, w2 = pl.pallas_call(
         lambda *refs: decode_kernel(*refs, NT=NT, HP=HP, WP=WP, FT=FT, TH=TH, TW=TW),
         out_shape=(
-            pltpu.VMEM((width_count - 1, FT, TH, TW, C2), bf16),
+            sent,
             pltpu.VMEM((width_count, FT + 1, TH + 2, 2 * TW, 3 * C), bf16),
             pltpu.VMEM(conv2_weight.shape, bf16),
         ),
@@ -329,10 +347,26 @@
         conv2_weight,
     )
     cols, w2 = resident(cols), resident(w2)
-    moved = [
-        lax.ppermute(other[step - 1], "width", [(k, (k + step) % width_count) for k in range(width_count)])
-        for step in range(1, width_count)
-    ]
+
+    def exchange(other):
+        return [
+            lax.ppermute(other[step - 1], "width", [(k, (k + step) % width_count) for k in range(width_count)])
+            for step in range(1, width_count)
+        ]
+
+    def send(low):
+        return pl.pallas_call(
+            lambda *refs: send_kernel(*refs, low=low),
+            out_shape=sent,
+            in_specs=[smem, vmem, vmem],
+            out_specs=vmem,
+            compiler_params=pltpu.CompilerParams(vmem_limit_bytes=8 * 1024 * 1024),
+            name="send",
+        )(position, cols, w2)
+
+    moved_low = exchange(other)
+    other = send(span)
+    moved_high = exchange(other)
     result = pl.pallas_call(
         own_kernel,
         out_shape=pltpu.VMEM((FT, TH, TW, C2), f32),
@@ -342,8 +376,8 @@
         name="own",
     )(position, cols, w2)
     result = result + conv2_bias
-    for part in moved:
-        result = result + part.astype(f32)
+    for low, high in zip(moved_low, moved_high):
+        result = result + jnp.concatenate([low, high], axis=-1).astype(f32)
     return result.astype(bf16)
 
 
@@ -364,7 +398,7 @@
 
     shape = (FRAMES * mesh.shape["tm"], ROWS * mesh.shape["height"], COLS * mesh.shape["width"])
     return jax.shard_map(
-        lambda *args: per_device(*args, clip=shape),
+        lambda *args: decode(*args, clip=shape),
         mesh=mesh,
         in_specs=placed,
         out_specs=P("tm", "height", "width", None),

time: 38 us -> 38.5 us (1.013)
  waiting for transfers between devices: 12.4 us -> 11.5 us
  starting transfers between devices: 8.6 us -> 9.42 us
  Pallas kernels: 13.5 us -> 14.1 us
    ppermute x1 -> x2, starting transfers between devices: 1.27 us -> 2.09 us  [exchange(): lax.ppermute(other[step - 1], 'width', [(k, (k + step) % width_count) for...]
    ppermute x1 -> x2, waiting for transfers between devices: 4.41 us -> 3.59 us  [exchange(): lax.ppermute(other[step - 1], 'width', [(k, (k + step) % width_count) for...]
    pallas_call x3 -> x4, Pallas kernels: 13.4 us -> 13.9 us  [the longest x1 7.17 us: decode(): pl.pallas_call(lambda *refs: decode_kernel(*refs, NT=NT, HP=HP, WP=WP, FT...]
  transfers between devices with their start and end apart: 2 -> 3, of which waited for: 2 -> 3; matrix products, arithmetic and copies ran while one was open for 6% -> 6% of each run, Pallas kernels for 7% -> 7%
where the time goes in v4:
time: 38.5 us; the launch traced here: 38.2 us
  Pallas kernels  14.1 us (37%)
  waiting for transfers between devices  11.5 us (30%)
  starting transfers between devices  9.42 us (24%)
  local copies, waits for them, and re-layouts  2.29 us (6%)
  other arithmetic  0.86 us (2%)
    all_to_all x1, waiting for transfers between devices, decode(): latent = lax.all_to_all(spread, AXES, 0, 0, tiled=True)  7.95 us
    all_to_all x1, starting transfers between devices, decode(): latent = lax.all_to_all(spread, AXES, 0, 0, tiled=True)  7.33 us
    pallas_call x1, Pallas kernels, decode(): pl.pallas_call(lambda *refs: decode_kernel(*refs, NT=NT, HP=HP, WP=WP, FT...  7.17 us
    ppermute x2, waiting for transfers between devices, exchange(): lax.ppermute(other[step - 1], 'width', [(k, (k + step) % width_count) for...  3.59 us
    pallas_call x1, Pallas kernels, project(): pl.pallas_call(project_kernel, out_shape=pltpu.VMEM((copies, count // 2,...  2.64 us
    pallas_call x1, Pallas kernels, decode(): pl.pallas_call(own_kernel, out_shape=pltpu.VMEM((FT, TH, TW, C2), f32), i...  2.52 us
    dynamic_slice x4, local copies, waits for them, and re-layouts, decode(): take = lambda x, axis: lax.dynamic_slice_in_dim(x, width * C, C, axis)  2.28 us
    ppermute x2, starting transfers between devices, exchange(): lax.ppermute(other[step - 1], 'width', [(k, (k + step) % width_count) for...  2.09 us
  transfers between devices with their start and end apart: 3, of which 3 were waited for; matrix products, arithmetic and copies ran while one was open for 6% of the time, Pallas kernels for 7%

profile of v4, /device:TPU:0, one launch (start us, length us, event | category | flops | bytes accessed | tf_op | source)
XLA Modules:
  0.0 38.2 jit_solution(15500989228570628882)
XLA Ops:
  0.0 0.0 copy-start
  0.0 2.6 %project.1 = bf16[32,32,128]{2,1,0:T(8,128)(2,1)} custom-call(bf16[64,3072]{1,0:T(8,128)(2,1)} %tok_ref.1, f32[1,3072]{1,0:T(1,128)} %bitcast.16, f32[1,3072]{1,0:T(1,128)} %bitcast.17, bf16[64,3072]{1,0:T(8,128)(2,1)} %weight_ref.1, f32[1,64]{1,0:T(1,128)} %bitcast.18), custom_call_target="tpu_custom_call" | custom-call | tf_op jit(solution)/shard_map/project/pallas_call | solution.py:41
  2.6 7.3 %all-to-all-start = ((bf16[32,32,128]{2,1,0:T(8,128)(2,1)}), bf16[32,32,128]{2,1,0:T(8,128)(2,1)S(1)}, u32[]{:S(2)}, u32[]{:S(2)}) async-start(bf16[32,32,128]{2,1,0:T(8,128)(2,1)} %project.1), calls=%async_computation | async-start | bytes 524288 | tf_op jit(solution)/shard_map/all_to_all | solution.py:309
  10.0 0.8 %dynamic_slice.13 = f32[256]{0:T(256)S(1)} dynamic-slice(f32[512]{0:T(512)} %param.17, s32[]{:T(128)S(6)} %select_n.2), dynamic_slice_sizes={256} | dynamic-slice | bytes 2052 | tf_op jit(solution)/shard_map/dynamic_slice | solution.py:314
  10.8 0.8 %dynamic_slice.14 = f32[256]{0:T(256)S(1)} dynamic-slice(f32[512]{0:T(512)} %param.18, s32[]{:T(128)S(6)} %select_n.2), dynamic_slice_sizes={256} | dynamic-slice | bytes 2052 | tf_op jit(solution)/shard_map/dynamic_slice | solution.py:314
  11.5 0.8 %dynamic_slice.15 = f32[256]{0:T(256)S(1)} dynamic-slice(f32[512]{0:T(512)} %param.19, s32[]{:T(128)S(6)} %select_n.2), dynamic_slice_sizes={256} | dynamic-slice | bytes 2052 | tf_op jit(solution)/shard_map/dynamic_slice | solution.py:314
  12.3 0.0 copy-done
  12.3 0.1 prepare.1
  12.4 0.1 pad_add_fusion.refs_0_.pos_ref
  12.5 7.9 %all-to-all-done.refs_1_ = bf16[32,32,128]{2,1,0:T(8,128)(2,1)S(1)} async-done(((bf16[32,32,128]{2,1,0:T(8,128)(2,1)}), bf16[32,32,128]{2,1,0:T(8,128)(2,1)S(1)}, u32[]{:S(2)}, u32[]{:S(2)}) %all-to-all-start) | async-done | bytes 262176 | tf_op jit(solution)/shard_map/all_to_all | solution.py:309
  20.4 7.2 %decode.1 = (bf16[1,4,8,8,256]{4,3,2,1,0:T(8,128)(2,1)S(1)}, bf16[2,5,10,16,768]{4,3,2,1,0:T(8,128)(2,1)S(1)}, bf16[3,3,3,256,512]{4,3,2,1,0:T(8,128)(2,1)S(1)}) custom-call(s32[3]{0:T(128)S(1)} %pad_add_fusion.refs_0_.pos_ref, bf16[32,32,128]{2,1,0:T(8,128)(2,1)S(1)} %all-to-all-done.refs_1_, bf16[768,1024]{1,0:T(8,128)(2,1)S(1)} %get-tuple-element.10.refs_2_, ...), custom_call_target="tpu_custom_call" | custom-call | tf_op jit(solution)/shard_map/decode/pallas_call | solution.py:325
  27.6 1.6 %send.1 = bf16[1,4,8,8,256]{4,3,2,1,0:T(8,128)(2,1)S(1)} custom-call(s32[3]{0:T(128)S(1)} %pad_add_fusion.refs_0_.pos_ref, bf16[2,5,10,16,768]{4,3,2,1,0:T(8,128)(2,1)S(1)} %get-tuple-element.12.cols.refs_1_, bf16[3,3,3,256,512]{4,3,2,1,0:T(8,128)(2,1)S(1)} %get-tuple-element.13.w2_ref.refs_2_), custom_call_target="tpu_custom_call" | custom-call | tf_op jit(solution)/shard_map/send/pallas_call | solution.py:358
  29.2 0.0 copy-start.1
  29.2 1.3 %collective-permute-start.1 = (bf16[4,8,8,256]{3,2,1,0:T(8,128)(2,1)S(1)}, bf16[4,8,8,256]{3,2,1,0:T(8,128)(2,1)S(1)}, u32[]{:S(2)}, u32[]{:S(2)}) collective-permute-start(bf16[4,8,8,256]{3,2,1,0:T(8,128)(2,1)S(1)} %bitcast.11), channel_id=1, source_target_pairs={{0,1},{1,0},{2,3},{3,2},{4,5},{5,4},{6,7},{7,6},{8,9},{9,8},{10,11... | collective-permute-start | bytes 393224 | tf_op jit(solution)/shard_map/ppermute | solution.py:353
  30.5 0.8 %collective-permute-start = (bf16[4,8,8,256]{3,2,1,0:T(8,128)(2,1)S(1)}, bf16[4,8,8,256]{3,2,1,0:T(8,128)(2,1)S(1)}, u32[]{:S(2)}, u32[]{:S(2)}) collective-permute-start(bf16[4,8,8,256]{3,2,1,0:T(8,128)(2,1)S(1)} %bitcast.15), channel_id=1, source_target_pairs={{0,1},{1,0},{2,3},{3,2},{4,5},{5,4},{6,7},{7,6},{8,9},{9,8},{10,11... | collective-permute-start | bytes 393224 | tf_op jit(solution)/shard_map/ppermute | solution.py:353
  31.3 2.5 %own.1 = f32[4,8,8,512]{3,2,1,0:T(8,128)S(1)} custom-call(s32[3]{0:T(128)S(1)} %pad_add_fusion.refs_0_.pos_ref, bf16[2,5,10,16,768]{4,3,2,1,0:T(8,128)(2,1)S(1)} %get-tuple-element.12.cols.refs_1_, bf16[3,3,3,256,512]{4,3,2,1,0:T(8,128)(2,1)S(1)} %get-tuple-element.13.w2_ref.refs_2_), custom_call_target="tpu_custom_call" | custom-call | tf_op jit(solution)/shard_map/own/pallas_call | solution.py:370
  33.9 1.8 %collective-permute-done.1 = bf16[4,8,8,256]{3,2,1,0:T(8,128)(2,1)S(1)} collective-permute-done((bf16[4,8,8,256]{3,2,1,0:T(8,128)(2,1)S(1)}, bf16[4,8,8,256]{3,2,1,0:T(8,128)(2,1)S(1)}, u32[]{:S(2)}, u32[]{:S(2)}) %collective-permute-start.1) | collective-permute-done | bytes 131104 | tf_op jit(solution)/shard_map/ppermute | solution.py:353
  35.7 1.8 %collective-permute-done = bf16[4,8,8,256]{3,2,1,0:T(8,128)(2,1)S(1)} collective-permute-done((bf16[4,8,8,256]{3,2,1,0:T(8,128)(2,1)S(1)}, bf16[4,8,8,256]{3,2,1,0:T(8,128)(2,1)S(1)}, u32[]{:S(2)}, u32[]{:S(2)}) %collective-permute-start) | collective-permute-done | bytes 131104 | tf_op jit(solution)/shard_map/ppermute | solution.py:353
  37.5 0.0 copy-done.1
  37.5 0.8 %add_convert_fusion = bf16[4,8,8,512]{3,2,1,0:T(8,128)(2,1)} fusion(f32[4,8,8,512]{3,2,1,0:T(8,128)S(1)} %own.1, bf16[4,8,8,256]{3,2,1,0:T(8,128)(2,1)S(1)} %collective-permute-done.1, bf16[4,8,8,256]{3,2,1,0:T(8,128)(2,1)S(1)} %collective-permute-done, f32[512]{0:T(512)S(1)} %copy-done.1), kind=kLoop, calls=%fused_computation | loop fusion | flops 917504 | bytes 1050624 | tf_op jit(solution)/shard_map/convert_element_type | solution.py:381
  (1 shorter events, 0.0 us)
Async XLA Ops:
  0.0 12.3 %copy-start = (bf16[3,3,3,16,512]{4,3,2,1,0:T(8,128)(2,1)S(1)}, bf16[3,3,3,16,512]{4,3,2,1,0:T(8,128)(2,1)}, u32[]{:S(2)}) copy-start(bf16[3,3,3,16,512]{4,3,2,1,0:T(8,128)(2,1)} %param.16) | copy-start | bytes 1327108
  2.6 17.8 %all-to-all-start = ((bf16[32,32,128]{2,1,0:T(8,128)(2,1)}), bf16[32,32,128]{2,1,0:T(8,128)(2,1)S(1)}, u32[]{:S(2)}, u32[]{:S(2)}) async-start(bf16[32,32,128]{2,1,0:T(8,128)(2,1)} %project.1), calls=%async_computation | async-start | bytes 524288 | tf_op jit(solution)/shard_map/all_to_all | solution.py:309
  29.2 8.2 %copy-start.1 = (f32[512]{0:T(512)S(1)}, f32[512]{0:T(512)}, u32[]{:S(2)}) copy-start(f32[512]{0:T(512)} %param.21) | copy-start | bytes 6148
  29.2 6.4 %collective-permute-start.1 = (bf16[4,8,8,256]{3,2,1,0:T(8,128)(2,1)S(1)}, bf16[4,8,8,256]{3,2,1,0:T(8,128)(2,1)S(1)}, u32[]{:S(2)}, u32[]{:S(2)}) collective-permute-start(bf16[4,8,8,256]{3,2,1,0:T(8,128)(2,1)S(1)} %bitcast.11), channel_id=1, source_target_pairs={{0,1},{1,0},{2,3},{3,2},{4,5},{5,4},{6,7},{7,6},{8,9},{9,8},{10,11... | collective-permute-start | bytes 393224 | tf_op jit(solution)/shard_map/ppermute | solution.py:353
  30.5 6.9 %collective-permute-start = (bf16[4,8,8,256]{3,2,1,0:T(8,128)(2,1)S(1)}, bf16[4,8,8,256]{3,2,1,0:T(8,128)(2,1)S(1)}, u32[]{:S(2)}, u32[]{:S(2)}) collective-permute-start(bf16[4,8,8,256]{3,2,1,0:T(8,128)(2,1)S(1)} %bitcast.15), channel_id=1, source_target_pairs={{0,1},{1,0},{2,3},{3,2},{4,5},{5,4},{6,7},{7,6},{8,9},{9,8},{10,11... | collective-permute-start | bytes 393224 | tf_op jit(solution)/shard_map/ppermute | solution.py:353

commit v5 on v4

--- a/solution.py
+++ b/solution.py
@@ -10,7 +10,8 @@
 FRAMES = 4
 ROWS = 8
 COLS = 8
-AXES = ("tm", "height", "width")
+AXES = ("ty", "tc", "height", "width")
+TIME = ("ty", "tc")
 bf16 = jnp.bfloat16
 f32 = jnp.float32
 
@@ -120,9 +121,79 @@
     store_tile(total, own_ref, FT // 2, TH, TW)
 
 
+def window_writer(rows, HP, WP, LAT):
+    frame_rows = HP * WP
+    LN = 8 * LAT
+    lane = lax.broadcasted_iota(jnp.int32, (rows, LN), 1)
+    q = lax.broadcasted_iota(jnp.int32, (rows, LN), 0) % WP
+    j_one = (lane // LAT) % 2 == 1
+    low = lane < LN // 2
+    keep = (j_one & (q > 0)) | (jnp.logical_not(j_one) & (q < WP - 1))
+    i_one = (lax.broadcasted_iota(jnp.int32, (frame_rows, LN), 1) // (2 * LAT)) % 2 == 1
+
+    def write(window, slot, latent_ref, first):
+        pieces = []
+        for k in range(frame_rows // (2 * rows)):
+            x = latent_ref[first + k].astype(f32)
+            z = jnp.where(j_one, pltpu.roll(x, 1, 0), pltpu.roll(x, rows - 1, 0))
+            z = jnp.where(keep, z, 0.0)
+            zr = pltpu.roll(z, LN // 2, 1)
+            xr = pltpu.roll(x, LN // 2, 1)
+            pieces.append(jnp.where(low, x, zr))
+            pieces.append(jnp.where(low, xr, z))
+        y = jnp.concatenate(pieces, axis=0)
+        zero = jnp.zeros((WP, LN), f32)
+        above = jnp.concatenate([zero, y[:-WP]], axis=0)
+        below = jnp.concatenate([y[WP:], zero], axis=0)
+        v = jnp.where(i_one, above, below)
+        window[slot, :, 0:LN] = y.astype(bf16)
+        window[slot, :, LN : 2 * LN] = v.astype(bf16)
+
+    return write
+
+
+def hidden_frames(frames, banded, bias, out, first, sums):
+    C = bias.shape[1]
+    s, sq = sums
+    for n in range(4):
+        taps = jnp.concatenate(
+            [jnp.concatenate([frame[a]() for frame in frames], axis=0) for a in range(3)], axis=1
+        )
+        h = jnp.dot(taps, banded[:, n * C : (n + 1) * C], preferred_element_type=f32) + bias
+        out[first : first + len(frames), :, :, n * C : (n + 1) * C] = h.reshape((len(frames),) + out.shape[1:3] + (C,))
+        h8 = h.reshape(h.shape[0] // 8, 8, C)
+        s = s + jnp.sum(h8, axis=0)
+        sq = sq + jnp.sum(h8 * h8, axis=0)
+    return s, sq
+
+
+def loader(window, slot):
+    return lambda: window[slot]
+
+
+def early_kernel(mine_ref, banded, affine, window, hidden, sums, *, HP, WP, FT):
+    TY = (window.shape[0] - 2) // FT
+    chunks = mine_ref.shape[0] // (TY * FT)
+    C = affine.shape[1]
+    write = window_writer(mine_ref.shape[1], HP, WP, banded.shape[0] // 48)
+    window[TY * FT :] = jnp.zeros((2,) + window.shape[1:], bf16)
+    totals = (jnp.zeros((8, C), f32), jnp.zeros((8, C), f32))
+    for ty in range(TY):
+        for k in range(FT):
+            write(window, ty * FT + k, mine_ref, (ty * FT + k) * chunks)
+    for ty in range(TY):
+        frames = [[loader(window, ty * FT + k + a - 2) for a in range(3)] for k in range(2, FT)]
+        totals = hidden_frames(frames, banded, affine[0:1, :], hidden, ty * (FT - 2), totals)
+    sums[0:8, :] = totals[0]
+    sums[8:16, :] = totals[1]
+
+
 def decode_kernel(
     pos_ref,
-    latent_ref,
+    theirs_ref,
+    window_mine,
+    hidden_early,
+    sums_early,
     banded,
     affine,
     w2_hbm,
@@ -142,70 +213,32 @@
     TW,
 ):
     C = w2_ref.shape[3]
-    LAT = banded.shape[0] // 48
     W = 2 * WP
     tm, height, width = pos_ref[0], pos_ref[1], pos_ref[2]
+    tc = tm % 2
     copy = pltpu.make_async_copy(w2_hbm, w2_ref, sem)
     copy.start()
 
-    rows = latent_ref.shape[1]
-    chunks = HP * WP // (2 * rows)
-    frame_rows = HP * WP
-    LN = 8 * LAT
-    window[0 : 2 * frame_rows, :] = jnp.zeros((2 * frame_rows, 2 * LN), bf16)
-    lane = lax.broadcasted_iota(jnp.int32, (rows, LN), 1)
-    q = lax.broadcasted_iota(jnp.int32, (rows, LN), 0) % WP
-    j_one = (lane // LAT) % 2 == 1
-    low = lane < LN // 2
-    keep = (j_one & (q > 0)) | (jnp.logical_not(j_one) & (q < WP - 1))
-    i_one = (lax.broadcasted_iota(jnp.int32, (frame_rows, LN), 1) // (2 * LAT)) % 2 == 1
-
-    def frame_body(t, carry):
-        pieces = []
-        for k in range(chunks):
-            x = latent_ref[t * chunks + k].astype(f32)
-            z = jnp.where(j_one, pltpu.roll(x, 1, 0), pltpu.roll(x, rows - 1, 0))
-            z = jnp.where(keep, z, 0.0)
-            zr = pltpu.roll(z, LN // 2, 1)
-            xr = pltpu.roll(x, LN // 2, 1)
-            pieces.append(jnp.where(low, x, zr))
-            pieces.append(jnp.where(low, xr, z))
-        y = jnp.concatenate(pieces, axis=0)
-        zero = jnp.zeros((WP, LN), f32)
-        above = jnp.concatenate([zero, y[:-WP]], axis=0)
-        below = jnp.concatenate([y[WP:], zero], axis=0)
-        v = jnp.where(i_one, above, below)
-        base = pl.multiple_of((t + 2) * frame_rows, frame_rows)
-        window[pl.ds(base, frame_rows), 0:LN] = y.astype(bf16)
-        window[pl.ds(base, frame_rows), LN : 2 * LN] = v.astype(bf16)
-        return carry
-
-    lax.fori_loop(0, NT, frame_body, 0, unroll=4)
-
-    FC = max(1, 2048 // frame_rows)
-    M = FC * frame_rows
-    bias = affine[0:1, :]
-    sums = []
-    squares = []
-    hidden[0:2] = jnp.zeros((2, HP, WP, 4 * C), f32)
-    for n in range(4):
-
-        def chunk_body(g, carry, n=n):
-            s, sq = carry
-            at = pl.multiple_of(g * M, M)
-            taps = jnp.concatenate(
-                [window[pl.ds(pl.multiple_of(at + a * frame_rows, frame_rows), M), :] for a in range(3)], axis=1
-            )
-            h = jnp.dot(taps, banded[:, n * C : (n + 1) * C], preferred_element_type=f32) + bias
-            hidden[pl.ds(g * FC + 2, FC), :, :, n * C : (n + 1) * C] = h.reshape(FC, HP, WP, C)
-            h8 = h.reshape(M // 8, 8, C)
-            return s + jnp.sum(h8, axis=0), sq + jnp.sum(h8 * h8, axis=0)
-
-        s, sq = lax.fori_loop(0, NT // FC, chunk_body, (jnp.zeros((8, C), f32), jnp.zeros((8, C), f32)))
-        sums.append(s)
-        squares.append(sq)
-    s = sums[0] + sums[1] + sums[2] + sums[3]
-    sq = squares[0] + squares[1] + squares[2] + squares[3]
+    TY = NT // (2 * FT)
+    chunks = theirs_ref.shape[0] // (TY * FT)
+    write = window_writer(theirs_ref.shape[1], HP, WP, banded.shape[0] // 48)
+    window[TY * FT :] = jnp.zeros((2,) + window.shape[1:], bf16)
+    for ty in range(TY):
+        for k in range(FT):
+            write(window, ty * FT + k, theirs_ref, (ty * FT + k) * chunks)
+
+    s, sq = sums_early[0:8, :], sums_early[8:16, :]
+    for ty in range(TY):
+        same = ty * FT + FT - 2
+        previous = (ty - 1) * FT + FT - 2 if ty > 0 else TY * FT
+        before_mine = jnp.where(tc == 1, same, previous)
+        before_theirs = jnp.where(tc == 1, previous, same)
+        sequence_mine = [loader(window, before_mine + k) for k in range(2)]
+        sequence_mine += [loader(window_mine, ty * FT + k) for k in range(2)]
+        sequence_theirs = [loader(window_mine, before_theirs + k) for k in range(2)]
+        sequence_theirs += [loader(window, ty * FT + k) for k in range(FT)]
+        frames = [sequence_theirs[k : k + 3] for k in reversed(range(FT))] + [sequence_mine[k : k + 3] for k in range(2)]
+        s, sq = hidden_frames(frames, banded, affine[0:1, :], hidden, ty * (FT + 2), (s, sq))
     s = jnp.broadcast_to(jnp.sum(s, axis=0, keepdims=True), (8, C))
     sq = jnp.broadcast_to(jnp.sum(sq, axis=0, keepdims=True), (8, C))
     size = C * lax.axis_size("width") // GROUPS
@@ -227,18 +260,27 @@
     first = height * (TH // 2) - 1
 
     def act_body(t, carry):
-        frame = tm * FT + t
+        actual = tm * FT + t - 2
+        frame = jnp.maximum(actual, 0)
+        group, k = frame // FT, frame % FT
+        mine = group % 2 == tc
+        early = mine & (k >= 2)
+        slot_early = (group // 2) * (FT - 2) + jnp.maximum(k - 2, 0)
+        slot = (group // 2) * (FT + 2) + jnp.where(mine, FT + jnp.minimum(k, 1), FT - 1 - k)
         for pp in range(TH // 2 + 2):
             prow = first + pp
             source = jnp.clip(prow, 0, HP - 1)
-            inside = (frame >= 2) & (prow >= 0) & (prow < HP)
+            inside = (actual >= 0) & (prow >= 0) & (prow < HP)
             for oi in range(2):
                 row = 2 * pp + oi - 1
                 if row < 0 or row >= R:
                     continue
                 for oj in range(2):
                     at = (oi * 2 + oj) * C
-                    h = hidden[frame, source, :, at : at + C].astype(bf16).astype(f32)
+                    h = jnp.where(
+                        early, hidden_early[slot_early, source, :, at : at + C], hidden[slot, source, :, at : at + C]
+                    )
+                    h = h.astype(bf16).astype(f32)
                     half = (h - gmean) * slope + offset
                     act = half * jnp.tanh(half) + half
                     act = jnp.where(inside, act, 0.0)
@@ -296,7 +338,7 @@
 ):
     width_count = lax.axis_size("width")
     height_count = lax.axis_size("height")
-    time_count = lax.axis_size("tm")
+    time_count = lax.axis_size(TIME)
     devices = width_count * height_count * time_count
     NT, NH, NW = clip
     FT, TH, TW = FRAMES, ROWS, COLS
@@ -305,21 +347,36 @@
     C = conv2_weight.shape[3]
     LAT = conv1_weight.shape[3]
 
-    spread = project(tokens, shift_mod, scale_mod, proj_weight, proj_bias, devices)
-    latent = lax.all_to_all(spread, AXES, 0, 0, tiled=True)
-    latent = pltpu.with_memory_space_constraint(latent, pltpu.VMEM)
+    spread = project(tokens, shift_mod, scale_mod, proj_weight, proj_bias, devices // 2)
+    mine = lax.all_to_all(spread, ("ty", "height", "width"), 0, 0, tiled=True)
+    theirs = lax.ppermute(mine, "tc", [(0, 1), (1, 0)])
 
     width = lax.axis_index("width")
-    position = jnp.stack([lax.axis_index("tm"), lax.axis_index("height"), width]).astype(jnp.int32)
+    position = jnp.stack([lax.axis_index(TIME), lax.axis_index("height"), width]).astype(jnp.int32)
     take = lambda x, axis: lax.dynamic_slice_in_dim(x, width * C, C, axis)
     smem = pl.BlockSpec(memory_space=pltpu.SMEM)
     vmem = pl.BlockSpec(memory_space=pltpu.VMEM)
     resident = lambda x: pltpu.with_memory_space_constraint(x, pltpu.VMEM)
     conv2_weight = pltpu.with_memory_space_constraint(conv2_weight, pltpu.HBM)
+    mine, theirs = resident(mine), resident(theirs)
     banded, affine = prepare(
         take(conv1_weight, 4), take(conv1_bias, 0), take(norm_gain, 0), take(norm_bias, 0)
     )
     banded, affine = resident(banded), resident(affine)
+    TY = time_count // 2
+    window, hidden, sums = pl.pallas_call(
+        lambda *refs: early_kernel(*refs, HP=HP, WP=WP, FT=FT),
+        out_shape=(
+            pltpu.VMEM((TY * FT + 2, HP * WP, 16 * LAT), bf16),
+            pltpu.VMEM((TY * (FT - 2), HP, WP, 4 * C), f32),
+            pltpu.VMEM((16, C), f32),
+        ),
+        in_specs=[vmem, vmem, vmem],
+        out_specs=(vmem, vmem, vmem),
+        compiler_params=pltpu.CompilerParams(vmem_limit_bytes=12 * 1024 * 1024),
+        name="early",
+    )(mine, banded, affine)
+    window, hidden, sums = resident(window), resident(hidden), resident(sums)
     span = C2 // 2
     sent = pltpu.VMEM((width_count - 1, FT, TH, TW, span), bf16)
     other, cols, w2 = pl.pallas_call(
@@ -329,23 +386,17 @@
             pltpu.VMEM((width_count, FT + 1, TH + 2, 2 * TW, 3 * C), bf16),
             pltpu.VMEM(conv2_weight.shape, bf16),
         ),
-        in_specs=[smem, vmem, vmem, vmem, pl.BlockSpec(memory_space=pl.ANY)],
+        in_specs=[smem] + [vmem] * 6 + [pl.BlockSpec(memory_space=pl.ANY)],
         out_specs=(vmem, vmem, vmem),
         scratch_shapes=[
-            pltpu.VMEM(((NT + 2) * HP * WP, 16 * LAT), bf16),
-            pltpu.VMEM((NT + 2, HP, WP, 4 * C), f32),
+            pltpu.VMEM((TY * FT + 2, HP * WP, 16 * LAT), bf16),
+            pltpu.VMEM((TY * (FT + 2), HP, WP, 4 * C), f32),
             pltpu.VMEM((pl.cdiv(C, 128), (FT + 2) * (TH + 2), NW + 16, 128), f32),
             pltpu.SemaphoreType.DMA,
         ],
-        compiler_params=pltpu.CompilerParams(vmem_limit_bytes=40 * 1024 * 1024),
+        compiler_params=pltpu.CompilerParams(vmem_limit_bytes=28 * 1024 * 1024),
         name="decode",
-    )(
-        position,
-        latent,
-        banded,
-        affine,
-        conv2_weight,
-    )
+    )(position, theirs, window, hidden, sums, banded, affine, conv2_weight)
     cols, w2 = resident(cols), resident(w2)
 
     def exchange(other):
@@ -397,10 +448,12 @@
     )
 
     shape = (FRAMES * mesh.shape["tm"], ROWS * mesh.shape["height"], COLS * mesh.shape["width"])
+    sizes = (mesh.shape["tm"] // 2, 2, mesh.shape["height"], mesh.shape["width"])
+    mesh = jax.sharding.Mesh(mesh.devices.reshape(sizes), AXES)
     return jax.shard_map(
         lambda *args: decode(*args, clip=shape),
         mesh=mesh,
         in_specs=placed,
-        out_specs=P("tm", "height", "width", None),
+        out_specs=P(TIME, "height", "width", None),
         check_vma=False,
     )

time: 38.5 us -> 39.6 us (1.029)
  starting transfers between devices: 9.42 us -> 10.4 us
  Pallas kernels: 14.1 us -> 13.6 us
  waiting for transfers between devices: 11.5 us -> 12 us
    pallas_call x1, Pallas kernels: 7.17 us -> 5.69 us  [decode(): pl.pallas_call(lambda *refs: decode_kernel(*refs, NT=NT, HP=HP, WP=WP, FT...]
    pallas_call x0 -> x1, Pallas kernels: none -> 1.12 us  [decode(): pl.pallas_call(lambda *refs: early_kernel(*refs, HP=HP, WP=WP, FT=FT), ou...]
    all_to_all x1, starting transfers between devices: 7.33 us -> 8.35 us  [decode(): mine = lax.all_to_all(spread, ('ty', 'height', 'width'), 0, 0, tiled=True)]
    ppermute x2, waiting for transfers between devices: 3.59 us -> 4.16 us  [exchange(): lax.ppermute(other[step - 1], 'width', [(k, (k + step) % width_count) for...]
  transfers between devices with their start and end apart: 3 -> 4, of which waited for: 3 -> 3; matrix products, arithmetic and copies ran while one was open for 6% -> 6% of each run, Pallas kernels for 7% -> 10%
where the time goes in v5:
time: 39.6 us; the launch traced here: 39.3 us
  Pallas kernels  13.6 us (34%)
  waiting for transfers between devices  12 us (30%)
  starting transfers between devices  10.4 us (26%)
  local copies, waits for them, and re-layouts  2.29 us (6%)
  other arithmetic  0.86 us (2%)
    all_to_all x1, starting transfers between devices, decode(): mine = lax.all_to_all(spread, ('ty', 'height', 'width'), 0, 0, tiled=True)  8.35 us
    all_to_all x1, waiting for transfers between devices, decode(): mine = lax.all_to_all(spread, ('ty', 'height', 'width'), 0, 0, tiled=True)  7.79 us
    pallas_call x1, Pallas kernels, decode(): pl.pallas_call(lambda *refs: decode_kernel(*refs, NT=NT, HP=HP, WP=WP, FT...  5.69 us
    ppermute x2, waiting for transfers between devices, exchange(): lax.ppermute(other[step - 1], 'width', [(k, (k + step) % width_count) for...  4.16 us
    pallas_call x1, Pallas kernels, project(): pl.pallas_call(project_kernel, out_shape=pltpu.VMEM((copies, count // 2,...  2.59 us
    pallas_call x1, Pallas kernels, decode(): pl.pallas_call(own_kernel, out_shape=pltpu.VMEM((FT, TH, TW, C2), f32), i...  2.52 us
    dynamic_slice x4, local copies, waits for them, and re-layouts, decode(): take = lambda x, axis: lax.dynamic_slice_in_dim(x, width * C, C, axis)  2.28 us
    ppermute x2, starting transfers between devices, exchange(): lax.ppermute(other[step - 1], 'width', [(k, (k + step) % width_count) for...  2.09 us
  transfers between devices with their start and end apart: 4, of which 3 were waited for; matrix products, arithmetic and copies ran while one was open for 6% of the time, Pallas kernels for 10%

profile of v5, /device:TPU:0, one launch (start us, length us, event | category | flops | bytes accessed | tf_op | source)
XLA Modules:
  0.0 39.3 jit_solution(11967716845299369707)
XLA Ops:
  0.0 0.0 copy-start
  0.0 2.6 %project.1 = bf16[16,32,128]{2,1,0:T(8,128)(2,1)} custom-call(bf16[64,3072]{1,0:T(8,128)(2,1)} %tok_ref.1, f32[1,3072]{1,0:T(1,128)} %bitcast.16, f32[1,3072]{1,0:T(1,128)} %bitcast.17, bf16[64,3072]{1,0:T(8,128)(2,1)} %weight_ref.1, f32[1,64]{1,0:T(1,128)} %bitcast.18), custom_call_target="tpu_custom_call" | custom-call | tf_op jit(solution)/shard_map/project/pallas_call | solution.py:42
  2.6 8.3 %all-to-all-start = ((bf16[16,32,128]{2,1,0:T(8,128)(2,1)}), bf16[16,32,128]{2,1,0:T(8,128)(2,1)S(1)}, u32[]{:S(2)}, u32[]{:S(2)}) async-start(bf16[16,32,128]{2,1,0:T(8,128)(2,1)} %project.1), calls=%async_computation | async-start | bytes 262144 | tf_op jit(solution)/shard_map/all_to_all | solution.py:351
  11.0 7.8 %all-to-all-done.refs_0_ = bf16[16,32,128]{2,1,0:T(8,128)(2,1)S(1)} async-done(((bf16[16,32,128]{2,1,0:T(8,128)(2,1)}), bf16[16,32,128]{2,1,0:T(8,128)(2,1)S(1)}, u32[]{:S(2)}, u32[]{:S(2)}) %all-to-all-start) | async-done | bytes 131104 | tf_op jit(solution)/shard_map/all_to_all | solution.py:351
  18.7 0.0 collective-permute-start
  18.7 0.0 copy-done
  18.8 0.8 %dynamic_slice.13 = f32[256]{0:T(256)S(1)} dynamic-slice(f32[512]{0:T(512)} %param.17, s32[]{:T(128)S(6)} %select_n.2), dynamic_slice_sizes={256} | dynamic-slice | bytes 2052 | tf_op jit(solution)/shard_map/dynamic_slice | solution.py:356
  19.5 0.8 %dynamic_slice.14 = f32[256]{0:T(256)S(1)} dynamic-slice(f32[512]{0:T(512)} %param.18, s32[]{:T(128)S(6)} %select_n.2), dynamic_slice_sizes={256} | dynamic-slice | bytes 2052 | tf_op jit(solution)/shard_map/dynamic_slice | solution.py:356
  20.3 0.8 %dynamic_slice.15 = f32[256]{0:T(256)S(1)} dynamic-slice(f32[512]{0:T(512)} %param.19, s32[]{:T(128)S(6)} %select_n.2), dynamic_slice_sizes={256} | dynamic-slice | bytes 2052 | tf_op jit(solution)/shard_map/dynamic_slice | solution.py:356
  21.0 0.1 prepare.1
  21.2 0.1 pad_add_fusion.refs_0_.pos_ref
  21.2 1.1 %early.1 = (bf16[10,128,256]{2,1,0:T(8,128)(2,1)S(1)}, f32[4,16,8,1024]{3,2,1,0:T(8,128)S(1)}, f32[16,256]{1,0:T(8,128)S(1)}) custom-call(bf16[16,32,128]{2,1,0:T(8,128)(2,1)S(1)} %all-to-all-done.refs_0_, bf16[768,1024]{1,0:T(8,128)(2,1)S(1)} %get-tuple-element.13.refs_1_.refs_5_, f32[3,256]{1,0:T(4,128)S(1)} %get-tuple-element.14.refs_2_.refs_6_), custom_call_target="tpu_custom_call" | custom-call | tf_op jit(solution)/shard_map/early/pallas_call | solution.py:367
  22.4 0.0 collective-permute-done.refs_1_
  22.4 5.7 %decode.1 = (bf16[1,4,8,8,256]{4,3,2,1,0:T(8,128)(2,1)S(1)}, bf16[2,5,10,16,768]{4,3,2,1,0:T(8,128)(2,1)S(1)}, bf16[3,3,3,256,512]{4,3,2,1,0:T(8,128)(2,1)S(1)}) custom-call(s32[3]{0:T(128)S(1)} %pad_add_fusion.refs_0_.pos_ref, bf16[16,32,128]{2,1,0:T(8,128)(2,1)S(1)} %collective-permute-done.refs_1_, bf16[10,128,256]{2,1,0:T(8,128)(2,1)S(1)} %get-tuple-element.15.refs_2_, ...), custom_call_target="tpu_custom_call" | custom-call | tf_op jit(solution)/shard_map/decode/pallas_call | solution.py:382
  28.1 1.6 %send.1 = bf16[1,4,8,8,256]{4,3,2,1,0:T(8,128)(2,1)S(1)} custom-call(s32[3]{0:T(128)S(1)} %pad_add_fusion.refs_0_.pos_ref, bf16[2,5,10,16,768]{4,3,2,1,0:T(8,128)(2,1)S(1)} %get-tuple-element.18.cols.refs_1_, bf16[3,3,3,256,512]{4,3,2,1,0:T(8,128)(2,1)S(1)} %get-tuple-element.19.w2_ref.refs_2_), custom_call_target="tpu_custom_call" | custom-call | tf_op jit(solution)/shard_map/send/pallas_call | solution.py:409
  29.7 1.1 %collective-permute-start.2 = (bf16[4,8,8,256]{3,2,1,0:T(8,128)(2,1)S(1)}, bf16[4,8,8,256]{3,2,1,0:T(8,128)(2,1)S(1)}, u32[]{:S(2)}, u32[]{:S(2)}) collective-permute-start(bf16[4,8,8,256]{3,2,1,0:T(8,128)(2,1)S(1)} %bitcast.11), channel_id=1, source_target_pairs={{0,1},{1,0},{2,3},{3,2},{4,5},{5,4},{6,7},{7,6},{8,9},{9,8},{10,11... | collective-permute-start | bytes 393224 | tf_op jit(solution)/shard_map/ppermute | solution.py:404
  30.9 0.0 copy-start.1
  30.9 0.9 %collective-permute-start.1 = (bf16[4,8,8,256]{3,2,1,0:T(8,128)(2,1)S(1)}, bf16[4,8,8,256]{3,2,1,0:T(8,128)(2,1)S(1)}, u32[]{:S(2)}, u32[]{:S(2)}) collective-permute-start(bf16[4,8,8,256]{3,2,1,0:T(8,128)(2,1)S(1)} %bitcast.15), channel_id=1, source_target_pairs={{0,1},{1,0},{2,3},{3,2},{4,5},{5,4},{6,7},{7,6},{8,9},{9,8},{10,11... | collective-permute-start | bytes 393224 | tf_op jit(solution)/shard_map/ppermute | solution.py:404
  31.8 2.5 %own.1 = f32[4,8,8,512]{3,2,1,0:T(8,128)S(1)} custom-call(s32[3]{0:T(128)S(1)} %pad_add_fusion.refs_0_.pos_ref, bf16[2,5,10,16,768]{4,3,2,1,0:T(8,128)(2,1)S(1)} %get-tuple-element.18.cols.refs_1_, bf16[3,3,3,256,512]{4,3,2,1,0:T(8,128)(2,1)S(1)} %get-tuple-element.19.w2_ref.refs_2_), custom_call_target="tpu_custom_call" | custom-call | tf_op jit(solution)/shard_map/own/pallas_call | solution.py:421
  34.3 1.8 %collective-permute-done.2 = bf16[4,8,8,256]{3,2,1,0:T(8,128)(2,1)S(1)} collective-permute-done((bf16[4,8,8,256]{3,2,1,0:T(8,128)(2,1)S(1)}, bf16[4,8,8,256]{3,2,1,0:T(8,128)(2,1)S(1)}, u32[]{:S(2)}, u32[]{:S(2)}) %collective-permute-start.2) | collective-permute-done | bytes 131104 | tf_op jit(solution)/shard_map/ppermute | solution.py:404
  36.1 2.3 %collective-permute-done.1 = bf16[4,8,8,256]{3,2,1,0:T(8,128)(2,1)S(1)} collective-permute-done((bf16[4,8,8,256]{3,2,1,0:T(8,128)(2,1)S(1)}, bf16[4,8,8,256]{3,2,1,0:T(8,128)(2,1)S(1)}, u32[]{:S(2)}, u32[]{:S(2)}) %collective-permute-start.1) | collective-permute-done | bytes 131104 | tf_op jit(solution)/shard_map/ppermute | solution.py:404
  38.5 0.0 copy-done.1
  38.5 0.8 %add_convert_fusion = bf16[4,8,8,512]{3,2,1,0:T(8,128)(2,1)} fusion(f32[4,8,8,512]{3,2,1,0:T(8,128)S(1)} %own.1, bf16[4,8,8,256]{3,2,1,0:T(8,128)(2,1)S(1)} %collective-permute-done.2, bf16[4,8,8,256]{3,2,1,0:T(8,128)(2,1)S(1)} %collective-permute-done.1, f32[512]{0:T(512)S(1)} %copy-done.1), kind=kLoop, calls=%fused_computation | loop fusion | flops 917504 | bytes 1050624 | tf_op jit(solution)/shard_map/convert_element_type | solution.py:432
  (1 shorter events, 0.0 us)
Async XLA Ops:
  0.0 18.7 %copy-start = (bf16[3,3,3,16,512]{4,3,2,1,0:T(8,128)(2,1)S(1)}, bf16[3,3,3,16,512]{4,3,2,1,0:T(8,128)(2,1)}, u32[]{:S(2)}) copy-start(bf16[3,3,3,16,512]{4,3,2,1,0:T(8,128)(2,1)} %param.16) | copy-start | bytes 1327108
  2.6 16.2 %all-to-all-start = ((bf16[16,32,128]{2,1,0:T(8,128)(2,1)}), bf16[16,32,128]{2,1,0:T(8,128)(2,1)S(1)}, u32[]{:S(2)}, u32[]{:S(2)}) async-start(bf16[16,32,128]{2,1,0:T(8,128)(2,1)} %project.1), calls=%async_computation | async-start | bytes 262144 | tf_op jit(solution)/shard_map/all_to_all | solution.py:351
  18.7 3.6 %collective-permute-start = (bf16[16,32,128]{2,1,0:T(8,128)(2,1)S(1)}, bf16[16,32,128]{2,1,0:T(8,128)(2,1)S(1)}, u32[]{:S(2)}, u32[]{:S(2)}) collective-permute-start(bf16[16,32,128]{2,1,0:T(8,128)(2,1)S(1)} %all-to-all-done.refs_0_), channel_id=1, source_target_pairs={{0,8},{8,0},{1,9},{9,1},{2,10},{10,2},{3,11},{11,3},{4,12},{12,4},... | collective-permute-start | bytes 393224 | tf_op jit(solution)/shard_map/ppermute | solution.py:352
  29.7 6.4 %collective-permute-start.2 = (bf16[4,8,8,256]{3,2,1,0:T(8,128)(2,1)S(1)}, bf16[4,8,8,256]{3,2,1,0:T(8,128)(2,1)S(1)}, u32[]{:S(2)}, u32[]{:S(2)}) collective-permute-start(bf16[4,8,8,256]{3,2,1,0:T(8,128)(2,1)S(1)} %bitcast.11), channel_id=1, source_target_pairs={{0,1},{1,0},{2,3},{3,2},{4,5},{5,4},{6,7},{7,6},{8,9},{9,8},{10,11... | collective-permute-start | bytes 393224 | tf_op jit(solution)/shard_map/ppermute | solution.py:404
  30.9 7.6 %copy-start.1 = (f32[512]{0:T(512)S(1)}, f32[512]{0:T(512)}, u32[]{:S(2)}) copy-start(f32[512]{0:T(512)} %param.21) | copy-start | bytes 6148
  30.9 7.6 %collective-permute-start.1 = (bf16[4,8,8,256]{3,2,1,0:T(8,128)(2,1)S(1)}, bf16[4,8,8,256]{3,2,1,0:T(8,128)(2,1)S(1)}, u32[]{:S(2)}, u32[]{:S(2)}) collective-permute-start(bf16[4,8,8,256]{3,2,1,0:T(8,128)(2,1)S(1)} %bitcast.15), channel_id=1, source_target_pairs={{0,1},{1,0},{2,3},{3,2},{4,5},{5,4},{6,7},{7,6},{8,9},{9,8},{10,11... | collective-permute-start | bytes 393224 | tf_op jit(solution)/shard_map/ppermute | solution.py:404
